TPU v7x, 512 devices: a whole 4x8x8 slice. The times are simulated.
512 devices in a mesh: seg: 32 (over y_lo, x, core), head: 16 (over z, y_hi).
Axes of the slice: x: 4, y: 8 (y_hi: 2, y_lo: 4; y = y_hi * 4 + y_lo), z: 8, core: 2. Of those that a mesh axis runs over, the one named last changes fastest.
Arguments:
- attn_query: bfloat16 [8, 4096, 3072], P(None, 'seg', 'head'), may hold values from -8 to 8
- attn_key: bfloat16 [8, 4096, 3072], P(None, 'seg', 'head'), may hold values from -8 to 8
- attn_value: bfloat16 [8, 4096, 3072], P(None, 'seg', 'head'), may hold values from -6 to 6
- prompt_len: int32 [8, 32], P(None, 'seg'), may hold values from 1 to 64, as said below
- ttt_weight: bfloat16 [3072, 9216], P(None, 'head'), may hold values from -0.109375 to 0.109375
- init_w1: float32 [48, 64, 256], P('head'), may hold values from -0.75 to 0.75
- init_w2t: float32 [48, 64, 256], P('head'), may hold values from -0.375 to 0.375
- step_rate: float32 [8, 48, 4096], P(None, 'head', 'seg'), may hold values from 0.005 to 0.05
Outputs:
- ttt_out: bfloat16 [8, 4096, 3072], P(None, 'seg', 'head')
Inputs may be any that keep to these rules, and one draw needn't show every extreme that they name: `prompt_len`: some entry equals 64.
All inputs are finite; a program needn't handle non-finite values.
Results may differ from a plain program's by a relative error of at most 0.008.
Values may be sent and summed in bfloat16 or wider, within the bound.
A program may use at most 64 MiB of HBM per device.

v0:
```python
import jax
import jax.numpy as jnp
from jax import lax
from jax.sharding import Mesh
from jax.sharding import PartitionSpec as P

MINI = 64
TEXT_SLOTS = 64
HEAD = ("head_0", "head_1")
SEG = ("seg_0", "seg_1", "seg_2")


highest_precision = lax.Precision.HIGHEST
norm_epsilon = 1e-05
rms_epsilon = 1e-06


def gathered_by_axis(value, axes, dim):
    out = value
    for number in range(len(axes) - 1, -1, -1):
        out = lax.all_gather(out, axes[number], axis=dim, tiled=True)
    return out


def cut_along(value, dim, length):
    before, after = (value.shape[:dim], value.shape[dim + 1 :])
    return jnp.moveaxis(value.reshape(*before, length, -1, *after), dim, 0)


def edges_of(length, count):
    unit = 8 if length >= 8 * count else 1
    return [length // unit * k // count * unit for k in range(1, count)]


def in_order(pieces, dim):
    lengths = list(pieces.shape[1:])
    lengths[dim] *= pieces.shape[0]
    return jnp.moveaxis(pieces, 0, dim).reshape(lengths)


def exchange_in_pieces(value, axis, pieces, split_dim, concat_dim):
    blocks = cut_along(value, split_dim, lax.axis_size(axis))
    split_at = max(range(1, max(2, blocks.ndim - 1)), key=lambda d: blocks.shape[d])
    gathered = []
    for share in jnp.split(blocks, edges_of(blocks.shape[split_at], pieces), axis=split_at):
        if share.size:
            gathered.append(lax.all_to_all(share, axis, split_axis=0, concat_axis=0, tiled=True))
    return in_order(jnp.concatenate(gathered, axis=split_at), concat_dim)


def turned_blocks(pieces, axes, order):
    inside = pieces.shape[1:]
    out = pieces.reshape(*(lax.axis_size(a) for a in axes), *inside)
    for k in order:
        out = lax.all_to_all(out, axes[k], k, k, tiled=True)
    return out.reshape(-1, *inside)


def two_step_exchange(value, groups, order, split_dim, concat_dim):
    length = lax.axis_size(groups[0]) * lax.axis_size(groups[1])
    pieces = cut_along(value, split_dim, length)
    return in_order(turned_blocks(pieces, groups, order), concat_dim)


def normalize(values):
    center = values - jnp.mean(values, axis=-1, keepdims=True)
    spread = jnp.mean(center * center, axis=-1, keepdims=True)
    return center * lax.rsqrt(spread + norm_epsilon)


def fast_mlp(inputs, fast_weights):
    hidden = jax.nn.gelu(
        jnp.einsum("bmd,bdf->bmf", inputs, fast_weights[:, 0], precision=highest_precision),
        approximate=True,
    )
    return normalize(
        jnp.einsum("bmf,bdf->bmd", hidden, fast_weights[:, 1], precision=highest_precision)
    )


def minibatch(fast_weights, batch_items):
    queries, key_rows, value_rows, step_rates = batch_items
    target = value_rows - key_rows

    def loss_value(weights_now):
        error = fast_mlp(key_rows, weights_now) - target
        return 0.5 * jnp.sum(step_rates[:, :, None] * error * error) / step_rates.shape[-1]

    gradient = jax.grad(loss_value)(fast_weights)
    fast_weights = fast_weights - gradient
    return (fast_weights, queries + fast_mlp(queries, fast_weights))


def run_items(fast_weights, picked, step_rates):
    batch = picked.shape[0]
    seg_len = picked.shape[2]
    head_dim = picked.shape[3]
    block_count = seg_len // MINI

    def to_blocks(array):
        return array.reshape(batch, block_count, MINI, head_dim).transpose(1, 0, 2, 3)

    rate_blocks = step_rates.reshape(batch, block_count, MINI).transpose(1, 0, 2)
    fast_weights, outputs = lax.scan(
        minibatch,
        fast_weights,
        (to_blocks(picked[:, 0]), to_blocks(picked[:, 1]), to_blocks(picked[:, 2]), rate_blocks),
    )
    return (fast_weights, outputs.transpose(1, 0, 2, 3).reshape(batch, seg_len, head_dim))


def body(attn_query, attn_key, attn_value, prompt_len, ttt_weight, init_w1, init_w2t, step_rate):
    videos = attn_query.shape[0]
    seg_len = attn_query.shape[1]
    heads_dev = init_w1.shape[0]
    head_dim = init_w1.shape[1]
    position = lax.broadcasted_iota(jnp.int32, (videos, seg_len), 1)
    usable = (position >= TEXT_SLOTS) | (position < prompt_len)
    queries = attn_query.reshape(videos, seg_len, heads_dev, head_dim)
    key_rows = attn_key.reshape(videos, seg_len, heads_dev, head_dim)
    value_rows = attn_value.reshape(videos, seg_len, heads_dev, head_dim)
    scores = jnp.einsum(
        "vqhd,vkhd->vhqk", queries, key_rows, preferred_element_type=jnp.float32
    ) * head_dim ** (-0.5)
    scores = jnp.where(usable[:, None, None, :], scores, -1e30)
    largest = jnp.max(scores, axis=-1, keepdims=True)
    exponent = jnp.exp(scores - largest)
    weights = (exponent / jnp.sum(exponent, axis=-1, keepdims=True)).astype(jnp.bfloat16)
    attended = jnp.einsum(
        "vhqk,vkhd->vqhd", weights, value_rows, preferred_element_type=jnp.float32
    )
    attended = attended.astype(jnp.bfloat16).reshape(videos, seg_len, heads_dev * head_dim)
    features = gathered_by_axis(attended, HEAD, 2)
    feature_full = features.astype(jnp.float32)
    normed = (
        feature_full
        * lax.rsqrt(jnp.mean(feature_full * feature_full, axis=-1, keepdims=True) + rms_epsilon)
    ).astype(jnp.bfloat16)
    projected = jnp.dot(
        normed.reshape(videos * seg_len, normed.shape[2]),
        ttt_weight,
        preferred_element_type=jnp.float32,
    )
    projected = projected.reshape(videos, seg_len, heads_dev, 3, head_dim).transpose(0, 2, 3, 1, 4)
    step_rates = step_rate * usable[:, None, :].astype(jnp.float32)
    init_stack = jnp.stack([init_w1, init_w2t], axis=1)
    seg_count = lax.axis_size(SEG)
    item_count = videos * heads_dev
    per_device = (item_count + seg_count - 1) // seg_count
    padded = per_device * seg_count
    item_inputs = projected.reshape(item_count, 3, seg_len, head_dim)
    item_inputs = jnp.pad(item_inputs, ((0, padded - item_count), (0, 0), (0, 0), (0, 0)))
    item_rates = step_rates.reshape(item_count, 1, seg_len, 1)
    item_rates = jnp.pad(item_rates, ((0, padded - item_count), (0, 0), (0, 0), (0, 0)))
    sequences, rate_rows = (
        exchange_in_pieces(item_inputs.astype(jnp.bfloat16), SEG, 2, 0, 2).astype(
            item_inputs.dtype
        ),
        exchange_in_pieces(item_rates.astype(jnp.bfloat16), SEG, 2, 0, 2).astype(item_rates.dtype),
    )
    item_global = lax.axis_index(SEG) * per_device + jnp.arange(per_device, dtype=jnp.int32)
    head_of = item_global % heads_dev
    start = jnp.take(init_stack, head_of, axis=0)
    final_weights, outputs = run_items(
        start, sequences, rate_rows.reshape(per_device, sequences.shape[2])
    )
    returned = two_step_exchange(
        outputs.astype(jnp.bfloat16), (("seg_0", "seg_1"), "seg_2"), (1, 0), 1, 0
    ).astype(outputs.dtype)
    results = returned[:item_count].reshape(videos, heads_dev, seg_len, head_dim)
    results = results.transpose(0, 2, 1, 3).reshape(videos, seg_len, heads_dev * head_dim)
    return results.astype(jnp.bfloat16)


def solution(mesh):
    finer = Mesh(
        mesh.devices.reshape(4, 4, 2, 8, 2), ("seg_0", "seg_1", "seg_2", "head_0", "head_1")
    )
    in_specs = (
        P(None, SEG, HEAD),
        P(None, SEG, HEAD),
        P(None, SEG, HEAD),
        P(None, SEG),
        P(None, HEAD),
        P(HEAD, None, None),
        P(HEAD, None, None),
        P(None, HEAD, SEG),
    )
    out_specs = P(None, SEG, HEAD)
    return jax.shard_map(body, mesh=finer, in_specs=in_specs, out_specs=out_specs, check_vma=False)
```

profile of v0, /device:TPU:8, one launch (start us, length us, event | category | flops | bytes accessed | tf_op | source)
XLA Modules:
  0.0 803.3 jit_solution(16057162189446475416)
XLA Ops:
  7.4 3.8 fusion.97
  11.2 1.8 convolution_convert_fusion
  13.3 23.4 %all_gather.6 = bf16[8,128,384]{1,0,2:T(8,128)(2,1)} all-gather(bf16[8,128,192]{1,0,2:T(8,128)(2,1)S(1)} %copy.69), channel_id=1, replica_groups=mesh['seg_0'=4,'seg_1'=4,'seg_2'=2,'head_0'=8,'head_1'=2] {'head_1'}, dimensions={2}, use_global_device_ids=true | all-gather | bytes 1179648 | tf_op jit(solution)/shard_map/all_gather | solution.py:21
  38.1 7.6 all-to-all-start
  45.7 1.3 copy.67
  47.0 72.9 %all-gather.2.cloned.1.call-done = bf16[8,128,3072]{1,0,2:T(8,128)(2,1)} async-done(((bf16[8,128,384]{1,0,2:T(8,128)(2,1)}), bf16[8,128,3072]{1,0,2:T(8,128)(2,1)}) %all-gather.2.cloned.1.call-update) | async-done | bytes 6291472 | tf_op jit(solution)/shard_map/all_gather | solution.py:21
  120.0 5.7 fusion.73
  125.7 1.3 fusion.75
  127.0 3.8 fusion.79
  130.9 1.4 pad_bitcast_fusion
  132.2 7.8 all-to-all-start.1
  140.0 4.3 fusion.95
  144.3 2.6 copy.71
  146.9 3.8 reshape.432
  150.7 7.8 all-to-all-start.2
  158.5 2.6 copy.72
  161.1 3.8 reshape.430
  164.9 14.1 %all-to-all-done.2 = bf16[32,2,6144]{2,1,0:T(2,128)(2,1)} async-done(((bf16[32,2,6144]{2,1,0:T(2,128)(2,1)}), bf16[32,2,6144]{2,1,0:T(2,128)(2,1)}, u32[]{:S(2)}, u32[]{:S(2)}) %all-to-all-start.2) | async-done | bytes 786464 | tf_op jit(solution)/shard_map/all_to_all | solution.py:47
  179.1 5.7 all-to-all-start.3
  184.8 1.5 fusion.84
  187.9 3.8 reshape.433
  191.7 3.2 copy.73
  194.8 10.5 %all-to-all-done.3 = bf16[32,2,6144]{2,1,0:T(2,128)(2,1)} async-done(((bf16[32,2,6144]{2,1,0:T(2,128)(2,1)}), bf16[32,2,6144]{2,1,0:T(2,128)(2,1)}, u32[]{:S(2)}, u32[]{:S(2)}) %all-to-all-start.3) | async-done | bytes 786464 | tf_op jit(solution)/shard_map/all_to_all | solution.py:47
  205.3 3.8 reshape.431
  209.1 3.2 copy.74
  212.3 2.7 maximum_convert_fusion
  215.0 10.0 %slice_reduce_fusion = (f32[4096,64]{0,1:T(8,128)}, f32[4096,64]{0,1:T(8,128)}, f32[4096,64]{0,1:T(8,128)}) fusion(f32[1,3,4096,64]{2,0,3,1:T(1,128)S(1)} %bitcast.125), kind=kLoop, calls=%fused_computation.111 | loop fusion | bytes 6291456 | tf_op jit(solution)/shard_map/slice | solution.py:107
  224.9 3.1 transpose_reshape_squeeze.10
  228.0 3.1 transpose_reshape_squeeze.11
  231.1 3.1 transpose_reshape_squeeze.9
  234.2 529.2 %while.15 = (s32[]{:T(128)}, f32[1,2,64,256]{3,2,1,0:T(8,128)}, bf16[64,1,64,64]{2,3,1,0:T(8,128)(2,1)}, f32[64,1,64]{2,1,0:T(1,128)}, f32[64,1,64,64]{2,0,3,1:T...) while((s32[]{:T(128)}, f32[1,2,64,256]{3,2,1,0:T(8,128)}, ...), condition=%wide.region_10.11_spmd, body=%wide.region_3.0_spmd.sunk | while | flops 88998464 | bytes 2877337 | solution.py:104
  239.4 1.1 fusion.132
  247.7 1.1 fusion.132
  297.4 1.1 fusion.132
  322.1 1.1 fusion.132
  330.3 1.1 fusion.132
  338.7 1.1 fusion.132
  355.2 1.1 fusion.132
  363.5 1.1 fusion.132
  404.8 1.1 fusion.132
  429.6 1.1 fusion.132
  437.9 1.1 fusion.132
  446.2 1.1 fusion.132
  454.5 1.1 fusion.132
  462.8 1.1 fusion.132
  471.1 1.1 fusion.132
  479.3 1.1 fusion.132
  495.8 1.1 fusion.132
  504.0 1.1 fusion.132
  553.6 1.1 fusion.132
  578.5 1.1 fusion.132
  611.5 1.1 fusion.132
  669.4 1.1 fusion.132
  677.7 1.1 fusion.132
  685.9 1.1 fusion.132
  710.8 1.1 fusion.132
  719.0 1.1 fusion.132
  735.6 1.1 fusion.132
  752.2 1.1 fusion.132
  763.4 2.9 copy.79
  766.3 2.9 convert_element_type.100
  769.2 1.1 copy.80
  770.3 4.6 all_to_all.30
  775.4 20.0 %all_to_all.31 = bf16[16,2,1,128,64]{3,1,4,2,0:T(2,128)(2,1)S(1)} all-to-all(bf16[16,2,1,128,64]{3,1,4,2,0:T(2,128)(2,1)S(1)} %copy.81), channel_id=1, replica_groups=mesh['seg_0'=4,'seg_1'=4,'seg_2'=2,'head_0'=8,'head_1'=2] {'seg_0','seg_1'}, dimensions={0} | all-to-all | bytes 1048576 | tf_op jit(solution)/shard_map/all_to_all | solution.py:55
  (1600 shorter events, 499.0 us)
Async XLA Ops:
  6.5 120.5 %copy-start = (bf16[3072,576]{0,1:T(8,128)(2,1)S(1)}, bf16[3072,576]{0,1:T(8,128)(2,1)}, u32[]{:S(2)}) copy-start(bf16[3072,576]{0,1:T(8,128)(2,1)} %param.14) | copy-start | bytes 10616836
  6.5 113.4 %all-gather.2.cloned.1.call-start = ((), (), s32[]{:S(2)}) async-start(), calls=%async_computation.6 | async-start | bytes 7077888 | tf_op jit(solution)/shard_map/all_gather | solution.py:21
  13.1 23.7 %copy-start.5 = (f32[8,3,128]{2,0,1:T(8,128)S(1)}, f32[8,3,128]{2,0,1:T(8,128)}, u32[]{:S(2)}) copy-start(f32[8,3,128]{2,0,1:T(8,128)} %param.17) | copy-start | bytes 36868
  38.1 94.2 %all-to-all-start = ((bf16[32,1,1,64,1]{3,4,2,1,0:T(2,128)(2,1)}), bf16[32,1,1,64,1]{3,4,2,1,0:T(2,128)(2,1)S(1)}, u32[]{:S(2)}, u32[]{:S(2)}) async-start(bf16[32,1,1,64,1]{3,4,2,1,0:T(2,128)(2,1)} %copy.66), calls=%async_computation | async-start | bytes 32768 | tf_op jit(solution)/shard_map/all_to_all | solution.py:47
  132.2 12.0 %copy-start.4 = (bf16[32,1,1,64,1]{3,4,2,1,0:T(2,128)(2,1)}, bf16[32,1,1,64,1]{3,4,2,1,0:T(2,128)(2,1)S(1)}, u32[]{:S(2)}) copy-start(bf16[32,1,1,64,1]{3,4,2,1,0:T(2,128)(2,1)S(1)} %all-to-all-done) | copy-start | bytes 12292
  132.2 18.5 %all-to-all-start.1 = ((bf16[32,1,1,64,1]{3,4,2,1,0:T(2,128)(2,1)}), bf16[32,1,1,64,1]{3,4,2,1,0:T(2,128)(2,1)}, u32[]{:S(2)}, u32[]{:S(2)}) async-start(bf16[32,1,1,64,1]{3,4,2,1,0:T(2,128)(2,1)} %copy.67), calls=%async_computation.1 | async-start | bytes 32768 | tf_op jit(solution)/shard_map/all_to_all | solution.py:47
  150.7 28.3 %all-to-all-start.2 = ((bf16[32,2,6144]{2,1,0:T(2,128)(2,1)}), bf16[32,2,6144]{2,1,0:T(2,128)(2,1)}, u32[]{:S(2)}, u32[]{:S(2)}) async-start(bf16[32,2,6144]{2,1,0:T(2,128)(2,1)} %reshape.432), calls=%async_computation.2 | async-start | bytes 1572864 | tf_op jit(solution)/shard_map/all_to_all | solution.py:47
  179.1 26.2 %all-to-all-start.3 = ((bf16[32,2,6144]{2,1,0:T(2,128)(2,1)}), bf16[32,2,6144]{2,1,0:T(2,128)(2,1)}, u32[]{:S(2)}, u32[]{:S(2)}) async-start(bf16[32,2,6144]{2,1,0:T(2,128)(2,1)} %reshape.430), calls=%async_computation.3 | async-start | bytes 1572864 | tf_op jit(solution)/shard_map/all_to_all | solution.py:47
  242.4 6.6 copy-start.2
  250.7 6.7 copy-start.2
  259.0 6.6 copy-start.2
  267.2 6.7 copy-start.2
  275.5 6.6 copy-start.2
  283.8 6.7 copy-start.2
  292.1 6.7 copy-start.2
  300.3 6.7 copy-start.2
  316.8 6.6 copy-start.2
  325.1 6.6 copy-start.2
  333.3 6.7 copy-start.2
  341.6 6.7 copy-start.2
  349.9 6.7 copy-start.2
  358.2 6.6 copy-start.2
  366.4 6.7 copy-start.2
  374.8 6.6 copy-start.2
  383.0 6.7 copy-start.2
  391.3 6.7 copy-start.2
  407.8 6.6 copy-start.2
  416.1 6.7 copy-start.2
  424.4 6.6 copy-start.2
  432.6 6.7 copy-start.2
  440.9 6.7 copy-start.2
  449.2 6.7 copy-start.2
  465.8 6.7 copy-start.2
  474.1 6.6 copy-start.2
  490.5 6.6 copy-start.2
  498.8 6.6 copy-start.2
  515.2 6.6 copy-start.2
  523.5 6.7 copy-start.2
  540.0 6.7 copy-start.2
  548.3 6.7 copy-start.2
  556.6 6.7 copy-start.2
  564.9 6.6 copy-start.2
  573.2 6.7 copy-start.2
  581.5 6.6 copy-start.2
  597.9 6.7 copy-start.2
  606.2 6.7 copy-start.2
  614.5 6.6 copy-start.2
  622.7 6.7 copy-start.2
  631.1 6.6 copy-start.2
  639.3 6.7 copy-start.2
  647.6 6.7 copy-start.2
  655.9 6.7 copy-start.2
  664.2 6.6 copy-start.2
  672.4 6.6 copy-start.2
  680.6 6.7 copy-start.2
  688.9 6.7 copy-start.2
  697.2 6.7 copy-start.2
  705.5 6.7 copy-start.2
  713.8 6.6 copy-start.2
  722.0 6.7 copy-start.2
  730.3 6.7 copy-start.2
  738.6 6.7 copy-start.2
  746.9 6.6 copy-start.2
  755.1 6.6 copy-start.2
  (73 other events, 100.7 us)
Sparse Core Ops, SparseCore 0:
  36.9 83.0 all-gather.1
where the time goes:
time: 817 us; the launch traced here: 803 us
  matrix products  280 us (34%)
  local copies, waits for them, and re-layouts  223 us (27%)
  other arithmetic  107 us (13%)
  waiting for transfers between devices  97.5 us (12%)
  blocking collectives  47.9 us (6%)
  starting transfers between devices  28.9 us (4%)
  between operations  13.6 us (2%)
    dot_general x256, matrix products, fast_mlp(): jnp.einsum('bmf,bdf->bmd', hidden, fast_weights[:, 1], precision=highest_...  169 us
    dynamic_slice x128, local copies, waits for them, and re-layouts, run_items(): lax.scan(minibatch, fast_weights, (to_blocks(picked[:, 0]), to_blocks(pic...  134 us
    dot_general x192, matrix products, fast_mlp(): jnp.einsum('bmd,bdf->bmf', inputs, fast_weights[:, 0], precision=highest_...  102 us
    all_gather x1, waiting for transfers between devices, gathered_by_axis(): out = lax.all_gather(out, axes[number], axis=dim, tiled=True)  72.9 us
    mul x64, other arithmetic, loss_value(): step_rates[:, :, None] * error * error  41 us
    dynamic_update_slice x64, other arithmetic, run_items(): lax.scan(minibatch, fast_weights, (to_blocks(picked[:, 0]), to_blocks(pic...  39.6 us
    all_to_all x4, starting transfers between devices, exchange_in_pieces(): lax.all_to_all(share, axis, split_axis=0, concat_axis=0, tiled=True)  28.9 us
    while x256, local copies, waits for them, and re-layouts  25.2 us
  transfers between devices with their start and end apart: 5, of which 3 were waited for; matrix products, arithmetic and copies ran while one was open for 5% of the time, Pallas kernels for 0%

commit v1 on v0

v1 whole, which is shorter than its diff:
```python
import math

import jax
import jax.numpy as jnp
from jax import lax
from jax.experimental import pallas as pl
from jax.experimental.pallas import tpu as pltpu
from jax.sharding import PartitionSpec as P

F32, BF = jnp.float32, jnp.bfloat16
GC = math.sqrt(2.0 / math.pi)
GA = 0.044715
VMEM_SPEC = pl.BlockSpec(memory_space=pltpu.VMEM)


def nn(a, b):
    return lax.dot_general(a, b, (((1,), (0,)), ((), ())), preferred_element_type=F32)


def nt(a, b):
    return lax.dot_general(a, b, (((1,), (1,)), ((), ())), preferred_element_type=F32)


def tn(a, b):
    return lax.dot_general(a, b, (((0,), (0,)), ((), ())), preferred_element_type=F32)


def attend(q, k, v, length, put):
    position = lax.broadcasted_iota(jnp.int32, (128, 1), 0)
    usable = (position >= 64) | (position < length)
    for h in range(3):
        cols = slice(64 * h, 64 * h + 64)
        scores = nt(k[:, cols], q[:, cols]) * 0.125
        scores = jnp.where(usable, scores, -1e30)
        exponent = jnp.exp(scores - jnp.max(scores, axis=0, keepdims=True))
        weights = (exponent * (1.0 / jnp.sum(exponent, axis=0, keepdims=True))).astype(BF)
        put(h, tn(v[:, cols], weights).astype(BF))


def attention_kernel(lengths, q, k, v, out):
    def put(h, value):
        out[0, 64 * h : 64 * h + 64, :] = value

    attend(q[0], k[0], v[0], lengths[pl.program_id(0), 0], put)


def attention(lengths, q, k, v):
    block = pl.BlockSpec((1, 128, 192), lambda i: (i, 0, 0))
    return pl.pallas_call(
        attention_kernel,
        grid=(8,),
        out_shape=jax.ShapeDtypeStruct((8, 192, 128), BF),
        in_specs=[pl.BlockSpec(memory_space=pltpu.SMEM), block, block, block],
        out_specs=pl.BlockSpec((1, 192, 128), lambda i: (i, 0, 0)),
        name="segment_attention",
    )(lengths, q, k, v)


def project_kernel(lengths, a, wt, rate, out):
    pair = pl.program_id(0)
    x = jnp.concatenate(
        [a[:, 0].reshape(3072, 128), a[:, 1].reshape(3072, 128)], axis=1
    ).astype(F32)
    scale = lax.rsqrt(jnp.mean(x * x, axis=0, keepdims=True) + 1e-6)
    normed = (x * scale).astype(BF)
    position = lax.broadcasted_iota(jnp.int32, (1, 128), 1)
    projected = nn(wt[...], normed).astype(BF)
    for half in range(2):
        usable = (position >= 64) | (position < lengths[2 * pair + half, 0])
        for h in range(3):
            item = 3 * half + h
            out[item, 0:192, :] = projected[192 * h : 192 * h + 192, 128 * half : 128 * half + 128]
            eta = jnp.where(usable, rate[half, h : h + 1, :], 0.0)
            out[item, 192:208, :] = jnp.broadcast_to(eta, (16, 128)).astype(BF)


def project(lengths, gathered, wt, rate):
    return pl.pallas_call(
        project_kernel,
        grid=(4,),
        out_shape=jax.ShapeDtypeStruct((24, 208, 128), BF),
        in_specs=[
            pl.BlockSpec(memory_space=pltpu.SMEM),
            pl.BlockSpec((16, 2, 192, 128), lambda i: (0, i, 0, 0)),
            pl.BlockSpec((576, 3072), lambda i: (0, 0)),
            pl.BlockSpec((2, 3, 128), lambda i: (i, 0, 0)),
        ],
        out_specs=pl.BlockSpec((6, 208, 128), lambda i: (i, 0, 0)),
        compiler_params=pltpu.CompilerParams(vmem_limit_bytes=48 << 20),
        name="norm_project",
    )(lengths, gathered, wt, rate)


def forward(u, w2b, xt, st):
    sq = u * u
    t = jnp.tanh(u * (GC + (GC * GA) * sq))
    half = 0.5 + 0.5 * t
    hb = (u * half).astype(BF)
    z = nn(w2b, hb)
    center = z - jnp.mean(z, axis=0, keepdims=True)
    rs = lax.rsqrt(jnp.mean(center * center, axis=0, keepdims=True) + 1e-5)
    y = center * rs
    return sq, t, half, hb, rs, y, y + (xt - st)


def scan_items(get, put, w1t0, w2t0, w2c0, w1s, w2s, w2ts, ub, xs, rprev, count):
    left = lax.broadcasted_iota(jnp.int32, (64, 128), 1) < 64
    left1 = lax.broadcasted_iota(jnp.int32, (1, 128), 1) < 64
    zero = jnp.zeros((64, 128), F32)
    zero1 = jnp.zeros((1, 128), F32)
    w1s[...] = w1t0[...]
    w2s[...] = w2t0[...]
    w2ts[...] = w2c0[...]
    x0 = jnp.where(left, get(0, 64, 64), zero)
    ub[...] = nn(w1s[...].astype(BF), x0.astype(BF))
    xs[...] = x0.T.astype(BF)

    def step(xt, st, eta, xnt):
        xntb = xnt.astype(BF)
        u = ub[...]
        sq, t, half, hb, rs, y, r = forward(u, w2s[...].astype(BF), xt, st)
        dy = r * (eta * (1.0 / 64.0))
        m1 = jnp.mean(dy, axis=0, keepdims=True)
        m2 = jnp.mean(dy * y, axis=0, keepdims=True)
        dzb = (rs * (dy - m1 - y * m2)).astype(BF)
        slope = half + (0.5 * u) * ((1.0 - t * t) * (GC + (3.0 * GC * GA) * sq))
        dub = (nn(w2ts[...].astype(BF), dzb) * slope).astype(BF)
        x = xs[...]
        w1 = w1s[...]
        ub[...] = nn(w1.astype(BF), xntb) - nn(dub, nn(x, xntb).astype(BF))
        w1s[...] = w1 - nn(dub, x)
        w2s[...] -= nt(dzb, hb)
        w2ts[...] -= nt(hb, dzb)
        xs[...] = xnt.T.astype(BF)
        return r

    def segment(s, carry):
        prev = jnp.maximum(s - 1, 0)
        qs, ks, vs = get(s, 0, 64), get(s, 64, 64), get(s, 128, 64)
        qp = get(prev, 0, 64)
        kn = get(jnp.minimum(s + 1, count - 1), 64, 64)
        rate = get(s, 192, 1)
        mid = jnp.where(left, qs, ks)
        even = step(
            jnp.where(left, ks, qp), jnp.where(left, vs, zero), jnp.where(left1, rate, zero1), mid
        )
        put(prev, jnp.where(left, rprev[...], even).astype(BF))
        rprev[...] = step(
            mid, jnp.where(left, zero, vs), jnp.where(left1, zero1, rate), jnp.where(left, kn, qs)
        )
        return carry

    rprev[...] = zero
    lax.fori_loop(0, count, segment, 0)
    last = forward(ub[...], w2s[...].astype(BF), get(count - 1, 0, 64), zero)[-1]
    put(count - 1, jnp.where(left, rprev[...], last).astype(BF))


SCAN_SCRATCH = [
    pltpu.VMEM((256, 64), F32),
    pltpu.VMEM((64, 256), F32),
    pltpu.VMEM((256, 64), F32),
    pltpu.VMEM((256, 128), F32),
    pltpu.VMEM((128, 64), BF),
    pltpu.VMEM((64, 128), F32),
]


def scan_kernel(qkv, w1t0, w2t0, w2c0, out, *scratch):
    def get(s, row, rows):
        return qkv[s, row : row + rows, :].astype(F32)

    def put(s, value):
        out[s] = value

    scan_items(get, put, w1t0, w2t0, w2c0, *scratch, qkv.shape[0])


def run_scan(qkv, w1t, w2t, w2c):
    return pl.pallas_call(
        scan_kernel,
        out_shape=jax.ShapeDtypeStruct((qkv.shape[0], 64, 128), BF),
        in_specs=[VMEM_SPEC] * 4,
        out_specs=VMEM_SPEC,
        scratch_shapes=SCAN_SCRATCH,
        name="ttt_scan",
    )(qkv, w1t, w2t, w2c)


def body(attn_query, attn_key, attn_value, prompt_len, ttt_weight, init_w1, init_w2t, step_rate):
    attended = attention(prompt_len, attn_query, attn_key, attn_value)
    gathered = lax.all_gather(attended, "head", axis=0)
    items = project(prompt_len, gathered, ttt_weight.T, step_rate)
    seg_count = lax.axis_size("seg")
    items = jnp.pad(items, ((0, seg_count - items.shape[0]), (0, 0), (0, 0)))
    sequence = lax.all_to_all(items, "seg", 0, 0, tiled=True)
    head = lax.axis_index("seg") % 3
    w1 = lax.dynamic_index_in_dim(init_w1, head, 0, keepdims=False)
    w2t = lax.dynamic_index_in_dim(init_w2t, head, 0, keepdims=False)
    outputs = run_scan(sequence, w1.T, w2t, w2t.T)
    returned = lax.all_to_all(outputs, "seg", 0, 0, tiled=True)
    returned = returned[:24].reshape(8, 192, 128)
    return jnp.swapaxes(returned, 1, 2)


def solution(mesh):
    in_specs = (
        P(None, "seg", "head"),
        P(None, "seg", "head"),
        P(None, "seg", "head"),
        P(None, "seg"),
        P(None, "head"),
        P("head", None, None),
        P("head", None, None),
        P(None, "head", "seg"),
    )
    return jax.shard_map(
        body, mesh=mesh, in_specs=in_specs, out_specs=P(None, "seg", "head"), check_vma=False
    )
```

time: 817 us -> 314 us (0.38)
  the two profiles are of different devices: /device:TPU:8 before, /device:TPU:1 now
where the time goes in v1:
time: 314 us; the launch traced here: 313 us
  waiting for transfers between devices  199 us (63%)
  Pallas kernels  53.7 us (17%)
  blocking collectives  22.9 us (7%)
  local copies, waits for them, and re-layouts  14.8 us (5%)
  between operations  13.5 us (4%)
  starting transfers between devices  9.25 us (3%)
    all_gather x1, waiting for transfers between devices, body(): gathered = lax.all_gather(attended, 'head', axis=0)  163 us
    pallas_call x1, Pallas kernels, run_scan(): pl.pallas_call(scan_kernel, out_shape=jax.ShapeDtypeStruct((qkv.shape[0],...  38.6 us
    all_to_all x1, waiting for transfers between devices, body(): sequence = lax.all_to_all(items, 'seg', 0, 0, tiled=True)  36.3 us
    all_to_all x1, blocking collectives, body(): returned = lax.all_to_all(outputs, 'seg', 0, 0, tiled=True)  22.9 us
    unnamed x17, local copies, waits for them, and re-layouts  9.65 us
    all_to_all x1, starting transfers between devices, body(): sequence = lax.all_to_all(items, 'seg', 0, 0, tiled=True)  9.25 us
    pallas_call x1, Pallas kernels, project(): pl.pallas_call(project_kernel, grid=(4,), out_shape=jax.ShapeDtypeStruct(...  7.68 us
    pallas_call x1, Pallas kernels, attention(): pl.pallas_call(attention_kernel, grid=(8,), out_shape=jax.ShapeDtypeStruc...  7.37 us
  transfers between devices with their start and end apart: 2, of which 2 were waited for; matrix products, arithmetic and copies ran while one was open for 1% of the time, Pallas kernels for 0%

profile of v1, /device:TPU:1, one launch (start us, length us, event | category | flops | bytes accessed | tf_op | source)
XLA Modules:
  0.0 313.3 jit_solution(5010530828194498255)
XLA Ops:
  6.5 0.0 copy-start
  6.5 0.0 copy-start.4
  6.5 0.0 all-gather.3.cloned.1.call-start
  6.5 1.4 copy.22.lengths
  7.9 2.0 copy.19.q
  9.9 2.0 copy.20.k
  11.9 0.0 copy-done.4
  11.9 0.0 copy-start.5
  11.9 0.0 copy-start.2
  11.9 1.1 copy.21.v
  13.0 7.4 %segment_attention.1 = bf16[8,192,128]{2,1,0:T(8,128)(2,1)} custom-call(s32[8,1]{1,0:T(8,128)} %copy.22.lengths, bf16[8,128,192]{2,1,0:T(8,128)(2,1)} %copy.19.q, bf16[8,128,192]{2,1,0:T(8,128)(2,1)} %copy.20.k, bf16[8,128,192]{2,1,0:T(8,128)(2,1)} %copy.21.v), custom_call_target="tpu_custom_call" | custom-call | tf_op jit(solution)/shard_map/segment_attention/pallas_call | solution.py:49
  20.3 0.0 all-gather.3.cloned.1.call-update
  20.4 0.0 copy-done.5
  20.4 162.8 %all-gather.3.cloned.1.call-done = bf16[128,192,128]{2,1,0:T(8,128)(2,1)} async-done(((bf16[8,192,128]{2,1,0:T(8,128)(2,1)}), bf16[128,192,128]{2,1,0:T(8,128)(2,1)}) %all-gather.3.cloned.1.call-update) | async-done | bytes 6291472 | tf_op jit(solution)/shard_map/all_gather | solution.py:192
  183.2 0.0 copy-done.2
  183.2 0.0 copy-start.1
  183.2 2.0 copy-done.1
  185.2 7.7 %norm_project.1 = bf16[24,208,128]{2,1,0:T(8,128)(2,1)S(1)} custom-call(s32[8,1]{1,0:T(8,128)S(1)} %copy-done.2, bf16[16,8,192,128]{3,2,1,0:T(8,128)(2,1)} %bitcast.14, bf16[576,3072]{1,0:T(8,128)(2,1)S(1)} %bitcast.13, f32[8,3,128]{2,1,0:T(4,128)S(1)} %copy.23.rate), custom_call_target="tpu_custom_call" | custom-call | tf_op jit(solution)/shard_map/norm_project/pallas_call | solution.py:78
  192.9 1.4 pad.4
  194.2 9.2 %all-to-all-start = ((bf16[32,208,128]{2,1,0:T(8,128)(2,1)}), bf16[32,208,128]{2,1,0:T(8,128)(2,1)S(1)}, u32[]{:S(2)}, u32[]{:S(2)}) async-start(bf16[32,208,128]{2,1,0:T(8,128)(2,1)} %pad.4), calls=%async_computation | async-start | bytes 3407872 | tf_op jit(solution)/shard_map/all_to_all | solution.py:196
  203.5 0.8 constant_dynamic-slice_fusion.1
  204.4 0.8 copy.24
  205.1 0.0 copy-done
  205.1 0.8 copy.25
  205.9 0.6 fusion.w2t0
  206.5 36.3 %all-to-all-done.qkv = bf16[32,208,128]{2,1,0:T(8,128)(2,1)S(1)} async-done(((bf16[32,208,128]{2,1,0:T(8,128)(2,1)}), bf16[32,208,128]{2,1,0:T(8,128)(2,1)S(1)}, u32[]{:S(2)}, u32[]{:S(2)}) %all-to-all-start) | async-done | bytes 1703968 | tf_op jit(solution)/shard_map/all_to_all | solution.py:196
  242.9 0.0 copy-start.3
  242.9 1.2 copy-done.3
  244.1 38.6 %ttt_scan.1 = bf16[32,64,128]{2,1,0:T(8,128)(2,1)} custom-call(bf16[32,208,128]{2,1,0:T(8,128)(2,1)} %copy-done.3, f32[256,64]{1,0:T(8,128)} %bitcast.15, f32[64,256]{1,0:T(8,128)} %fusion.w2t0, f32[256,64]{1,0:T(8,128)} %bitcast.16), custom_call_target="tpu_custom_call" | custom-call | tf_op jit(solution)/shard_map/ttt_scan/pallas_call | solution.py:180
  282.7 22.9 %all_to_all.10 = bf16[32,64,128]{2,1,0:T(8,128)(2,1)S(1)} all-to-all(bf16[32,64,128]{2,1,0:T(8,128)(2,1)} %ttt_scan.1), channel_id=1, replica_groups=mesh['seg'=32,'head'=16] {'seg'}, dimensions={0} | all-to-all | bytes 1048576 | tf_op jit(solution)/shard_map/all_to_all | solution.py:201
  305.7 0.8 slice.4
  (2 shorter events, 0.0 us)
Async XLA Ops:
  6.5 198.6 %copy-start = (f32[3,64,256]{2,1,0:T(8,128)S(1)}, f32[3,64,256]{2,1,0:T(8,128)}, u32[]{:S(2)}) copy-start(f32[3,64,256]{2,1,0:T(8,128)} %param.14) | copy-start | bytes 589828
  6.5 5.4 %copy-start.4 = (bf16[8,128,192]{1,2,0:T(8,128)(2,1)S(1)}, bf16[8,128,192]{1,2,0:T(8,128)(2,1)}, u32[]{:S(2)}) copy-start(bf16[8,128,192]{1,2,0:T(8,128)(2,1)} %param.10) | copy-start | bytes 1179652
  6.5 176.6 %all-gather.3.cloned.1.call-start = ((), (), s32[]{:S(2)}) async-start(), calls=%async_computation.2 | async-start | bytes 6684672 | tf_op jit(solution)/shard_map/all_gather | solution.py:192
  11.9 8.5 %copy-start.5 = (f32[8,3,128]{2,0,1:T(8,128)S(1)}, f32[8,3,128]{2,0,1:T(8,128)}, u32[]{:S(2)}) copy-start(f32[8,3,128]{2,0,1:T(8,128)} %param.15) | copy-start | bytes 36868
  11.9 171.3 %copy-start.2 = (s32[8,1]{1,0:T(8,128)S(1)}, s32[8,1]{1,0:T(8,128)}, u32[]{:S(2)}) copy-start(s32[8,1]{1,0:T(8,128)} %copy.22.lengths) | copy-start | bytes 100
  183.2 2.0 copy-start.1
  194.2 48.6 %all-to-all-start = ((bf16[32,208,128]{2,1,0:T(8,128)(2,1)}), bf16[32,208,128]{2,1,0:T(8,128)(2,1)S(1)}, u32[]{:S(2)}, u32[]{:S(2)}) async-start(bf16[32,208,128]{2,1,0:T(8,128)(2,1)} %pad.4), calls=%async_computation | async-start | bytes 3407872 | tf_op jit(solution)/shard_map/all_to_all | solution.py:196
  242.9 1.2 copy-start.3
Sparse Core Ops, SparseCore 0:
  20.5 162.6 all-gather.2

commit v2 on v1

--- a/solution.py
+++ b/solution.py
@@ -10,6 +10,7 @@
 F32, BF = jnp.float32, jnp.bfloat16
 GC = math.sqrt(2.0 / math.pi)
 GA = 0.044715
+MESH = pl.DeviceIdType.MESH
 VMEM_SPEC = pl.BlockSpec(memory_space=pltpu.VMEM)
 
 
@@ -29,66 +30,188 @@
     position = lax.broadcasted_iota(jnp.int32, (128, 1), 0)
     usable = (position >= 64) | (position < length)
     for h in range(3):
-        cols = slice(64 * h, 64 * h + 64)
-        scores = nt(k[:, cols], q[:, cols]) * 0.125
+        rows = slice(64 * h, 64 * h + 64)
+        scores = tn(k[rows, :], q[rows, :]) * 0.125
         scores = jnp.where(usable, scores, -1e30)
         exponent = jnp.exp(scores - jnp.max(scores, axis=0, keepdims=True))
         weights = (exponent * (1.0 / jnp.sum(exponent, axis=0, keepdims=True))).astype(BF)
-        put(h, tn(v[:, cols], weights).astype(BF))
-
-
-def attention_kernel(lengths, q, k, v, out):
-    def put(h, value):
-        out[0, 64 * h : 64 * h + 64, :] = value
-
-    attend(q[0], k[0], v[0], lengths[pl.program_id(0), 0], put)
-
-
-def attention(lengths, q, k, v):
-    block = pl.BlockSpec((1, 128, 192), lambda i: (i, 0, 0))
+        put(h, nn(v[rows, :], weights).astype(BF))
+
+
+def gather_kernel(
+    lengths, q, k, v, wt, rate, out, buf, acc, ssq, wv, wsem, psem, rsem, lsem, recv
+):
+    me = lax.axis_index("head")
+    z, y = me // 2, lax.rem(me, 2)
+    right, left, partner = lax.rem(me + 2, 16), lax.rem(me + 14, 16), 2 * z + 1 - y
+    barrier = pltpu.get_barrier_semaphore()
+    for peer in (right, left, partner):
+        pl.semaphore_signal(barrier, inc=1, device_id={"head": peer}, device_id_type=MESH)
+    pl.semaphore_wait(barrier, 3)
+    load = pltpu.make_async_copy(wt, wv, wsem)
+    load.start()
+
+    def copy(zo, c, yo, sem, peer):
+        return pltpu.make_async_remote_copy(
+            src_ref=buf.at[zo, c, yo],
+            dst_ref=buf.at[zo, c, yo],
+            send_sem=sem,
+            recv_sem=recv.at[zo, c, yo],
+            device_id={"head": peer},
+            device_id_type=MESH,
+        )
+
+    def to_right(zo, c, yo, d, o):
+        return copy(zo, c, yo, rsem.at[d, o, c], right)
+
+    def to_left(zo, c, yo, d, o):
+        return copy(zo, c, yo, lsem.at[d, o, c], left)
+
+    def send_own(c):
+        to_right(z, c, y, 0, 0).start()
+        to_left(z, c, y, 0, 0).start()
+        copy(z, c, y, psem.at[c], partner).start()
+
+    def attend_pair(c, carry):
+        for half in range(2):
+            video = 2 * c + half
+
+            def put(h, value):
+                buf[z, c, y, 64 * h : 64 * h + 64, 128 * half : 128 * half + 128] = value
+
+            attend(q[video], k[video], v[video], lengths[video, 0], put)
+
+        @pl.when(c > 0)
+        def _():
+            send_own(c - 1)
+
+        return carry
+
+    lax.fori_loop(0, 4, attend_pair, 0)
+    load.wait()
+
+    def add(zo, c):
+        x = buf[zo, c].reshape(384, 256)
+        w = wv[:, pl.ds(pl.multiple_of(zo * 384, 128), 384)]
+        acc[c] += nn(w, x)
+        xf = x.astype(F32)
+        ssq[c] += jnp.sum((xf * xf).reshape(48, 8, 256), axis=0)
+
+    def first(c, carry):
+        acc[c] = jnp.zeros((576, 256), F32)
+        ssq[c] = jnp.zeros((8, 256), F32)
+        copy(z, c, 1 - y, psem.at[c], partner).wait_recv()
+        to_right(z, c, 1 - y, 0, 1).start()
+        to_left(z, c, 1 - y, 0, 1).start()
+
+        @pl.when(c == 0)
+        def _():
+            send_own(3)
+
+        add(z, c)
+        return carry
+
+    lax.fori_loop(0, 4, first, 0)
+
+    def hop(d, carry):
+        zr, zl = lax.rem(z + 8 - d, 8), lax.rem(z + d, 8)
+        for o in range(2):
+            yo = y if o == 0 else 1 - y
+
+            def chunk(c, inner):
+                @pl.when((d < 4) | (c < 2))
+                def _():
+                    to_right(zr, c, yo, 0, 0).wait_recv()
+
+                @pl.when((d < 3) | ((d == 3) & (c < 2)))
+                def _():
+                    to_right(zr, c, yo, d, o).start()
+
+                @pl.when((d < 4) | (c >= 2))
+                def _():
+                    to_left(zl, c, yo, 0, 0).wait_recv()
+
+                @pl.when((d < 3) | ((d == 3) & (c >= 2)))
+                def _():
+                    to_left(zl, c, yo, d, o).start()
+
+                if o == 1:
+                    add(zl, c)
+
+                    @pl.when(d < 4)
+                    def _():
+                        add(zr, c)
+
+                return inner
+
+            lax.fori_loop(0, 4, chunk, 0)
+        return carry
+
+    lax.fori_loop(1, 5, hop, 0)
+
+    position = lax.broadcasted_iota(jnp.int32, (1, 128), 1)
+
+    def finish(c, carry):
+        mean = jnp.sum(ssq[c], axis=0, keepdims=True) * (1.0 / 3072.0)
+        projected = (acc[c] * lax.rsqrt(mean + 1e-6)).astype(BF)
+        for half in range(2):
+            video = 2 * c + half
+            usable = (position >= 64) | (position < lengths[video, 0])
+            for h in range(3):
+                item = video * 3 + h
+                out[item, 0:192, :] = projected[
+                    192 * h : 192 * h + 192, 128 * half : 128 * half + 128
+                ]
+                eta = jnp.where(usable, rate[h, pl.ds(video, 1), :], 0.0)
+                out[item, 192:208, :] = jnp.broadcast_to(eta, (16, 128)).astype(BF)
+        copy(z, c, y, psem.at[c], partner).wait_send()
+        for o in range(2):
+            for d in range(3):
+                to_right(z, c, y, d, o).wait_send()
+                to_left(z, c, y, d, o).wait_send()
+
+            @pl.when(c < 2)
+            def _():
+                to_right(z, c, y, 3, o).wait_send()
+
+            @pl.when(c >= 2)
+            def _():
+                to_left(z, c, y, 3, o).wait_send()
+
+        return carry
+
+    lax.fori_loop(0, 4, finish, 0)
+
+
+def gather_project(lengths, q, k, v, wt, rate):
     return pl.pallas_call(
-        attention_kernel,
-        grid=(8,),
-        out_shape=jax.ShapeDtypeStruct((8, 192, 128), BF),
-        in_specs=[pl.BlockSpec(memory_space=pltpu.SMEM), block, block, block],
-        out_specs=pl.BlockSpec((1, 192, 128), lambda i: (i, 0, 0)),
-        name="segment_attention",
-    )(lengths, q, k, v)
-
-
-def project_kernel(lengths, a, wt, rate, out):
-    pair = pl.program_id(0)
-    x = jnp.concatenate(
-        [a[:, 0].reshape(3072, 128), a[:, 1].reshape(3072, 128)], axis=1
-    ).astype(F32)
-    scale = lax.rsqrt(jnp.mean(x * x, axis=0, keepdims=True) + 1e-6)
-    normed = (x * scale).astype(BF)
-    position = lax.broadcasted_iota(jnp.int32, (1, 128), 1)
-    projected = nn(wt[...], normed).astype(BF)
-    for half in range(2):
-        usable = (position >= 64) | (position < lengths[2 * pair + half, 0])
-        for h in range(3):
-            item = 3 * half + h
-            out[item, 0:192, :] = projected[192 * h : 192 * h + 192, 128 * half : 128 * half + 128]
-            eta = jnp.where(usable, rate[half, h : h + 1, :], 0.0)
-            out[item, 192:208, :] = jnp.broadcast_to(eta, (16, 128)).astype(BF)
-
-
-def project(lengths, gathered, wt, rate):
-    return pl.pallas_call(
-        project_kernel,
-        grid=(4,),
+        gather_kernel,
         out_shape=jax.ShapeDtypeStruct((24, 208, 128), BF),
         in_specs=[
             pl.BlockSpec(memory_space=pltpu.SMEM),
-            pl.BlockSpec((16, 2, 192, 128), lambda i: (0, i, 0, 0)),
-            pl.BlockSpec((576, 3072), lambda i: (0, 0)),
-            pl.BlockSpec((2, 3, 128), lambda i: (i, 0, 0)),
+            VMEM_SPEC,
+            VMEM_SPEC,
+            VMEM_SPEC,
+            pl.BlockSpec(memory_space=pl.ANY),
+            VMEM_SPEC,
         ],
-        out_specs=pl.BlockSpec((6, 208, 128), lambda i: (i, 0, 0)),
-        compiler_params=pltpu.CompilerParams(vmem_limit_bytes=48 << 20),
-        name="norm_project",
-    )(lengths, gathered, wt, rate)
+        out_specs=VMEM_SPEC,
+        scratch_shapes=[
+            pltpu.VMEM((8, 4, 2, 192, 256), BF),
+            pltpu.VMEM((4, 576, 256), F32),
+            pltpu.VMEM((4, 8, 256), F32),
+            pltpu.VMEM((576, 3072), BF),
+            pltpu.SemaphoreType.DMA,
+            pltpu.SemaphoreType.DMA((4,)),
+            pltpu.SemaphoreType.DMA((4, 2, 4)),
+            pltpu.SemaphoreType.DMA((4, 2, 4)),
+            pltpu.SemaphoreType.DMA((8, 4, 2)),
+        ],
+        compiler_params=pltpu.CompilerParams(
+            collective_id=0, has_side_effects=True, vmem_limit_bytes=56 << 20
+        ),
+        name="attend_gather_project",
+    )(lengths, q, k, v, wt, rate)
 
 
 def forward(u, w2b, xt, st):
@@ -188,9 +311,17 @@
 
 
 def body(attn_query, attn_key, attn_value, prompt_len, ttt_weight, init_w1, init_w2t, step_rate):
-    attended = attention(prompt_len, attn_query, attn_key, attn_value)
-    gathered = lax.all_gather(attended, "head", axis=0)
-    items = project(prompt_len, gathered, ttt_weight.T, step_rate)
+    def turned(array):
+        return jnp.swapaxes(array, 1, 2)
+
+    items = gather_project(
+        prompt_len,
+        turned(attn_query),
+        turned(attn_key),
+        turned(attn_value),
+        ttt_weight.T,
+        jnp.swapaxes(step_rate, 0, 1),
+    )
     seg_count = lax.axis_size("seg")
     items = jnp.pad(items, ((0, seg_count - items.shape[0]), (0, 0), (0, 0)))
     sequence = lax.all_to_all(items, "seg", 0, 0, tiled=True)

time: 314 us -> 199 us (0.63)
  waiting for transfers between devices: 199 us -> 36.4 us
  Pallas kernels: 53.7 us -> 119 us
  between operations: 13.5 us -> 0.05 us
  local copies, waits for them, and re-layouts: 14.8 us -> 8.96 us
    all_gather x1 -> x0, waiting for transfers between devices: 163 us -> none  [body(): gathered = lax.all_gather(attended, 'head', axis=0)]
    pallas_call x2 -> x1, Pallas kernels: 15.1 us -> 80.7 us  [gather_project(): pl.pallas_call(gather_kernel, out_shape=jax.ShapeDtypeStruct((24, 208, 12...]
    unnamed x17 -> x5, local copies, waits for them, and re-layouts: 9.65 us -> 2.56 us
  transfers between devices with their start and end apart: 2 -> 1, of which waited for: 2 -> 1; matrix products, arithmetic and copies ran while one was open for 1% -> 2% of each run, Pallas kernels for 0% -> 0%
where the time goes in v2:
time: 199 us
  Pallas kernels  119 us (60%)
  waiting for transfers between devices  36.4 us (18%)
  blocking collectives  22.9 us (12%)
  starting transfers between devices  11.2 us (6%)
  local copies, waits for them, and re-layouts  8.96 us (5%)
    pallas_call x1, Pallas kernels, gather_project(): pl.pallas_call(gather_kernel, out_shape=jax.ShapeDtypeStruct((24, 208, 12...  80.7 us
    pallas_call x1, Pallas kernels, run_scan(): pl.pallas_call(scan_kernel, out_shape=jax.ShapeDtypeStruct((qkv.shape[0],...  38.6 us
    all_to_all x1, waiting for transfers between devices, body(): sequence = lax.all_to_all(items, 'seg', 0, 0, tiled=True)  36.4 us
    all_to_all x1, blocking collectives, body(): returned = lax.all_to_all(outputs, 'seg', 0, 0, tiled=True)  22.9 us
    all_to_all x1, starting transfers between devices, body(): sequence = lax.all_to_all(items, 'seg', 0, 0, tiled=True)  11.2 us
  transfers between devices with their start and end apart: 1, of which 1 were waited for; matrix products, arithmetic and copies ran while one was open for 2% of the time, Pallas kernels for 0%

profile of v2, /device:TPU:1, one launch (start us, length us, event | category | flops | bytes accessed | tf_op | source)
XLA Modules:
  0.0 198.8 jit_solution(3302409009249477512)
XLA Ops:
  0.0 0.0 copy-start
  0.0 1.4 copy.9.lengths
  1.4 80.7 %attend_gather_project.1 = bf16[24,208,128]{2,1,0:T(8,128)(2,1)} custom-call(s32[8,1]{1,0:T(8,128)} %copy.9.lengths, bf16[8,192,128]{2,1,0:T(8,128)(2,1)} %bitcast.19, bf16[8,192,128]{2,1,0:T(8,128)(2,1)} %bitcast.20, bf16[8,192,128]{2,1,0:T(8,128)(2,1)} %bitcast.21, bf16[576,3072]{1,0:T(8,128)(2,1)} %bitcast.16, f32[3,8,128]{2,1,0:T(8,128)} %bitcast.22), custom_call_target="tpu_custom_call" | custom-call | tf_op jit(solution)/shard_map/attend_gather_project/pallas_call | solution.py:187
  82.0 2.6 %pad.4 = bf16[32,208,128]{2,1,0:T(8,128)(2,1)} pad(bf16[24,208,128]{2,1,0:T(8,128)(2,1)} %attend_gather_project.1, bf16[]{:T(256)} %constant.20.clone.1), padding=0_8x0_0x0_0 | pad | bytes 2981890 | tf_op jit(solution)/shard_map/jit(_pad)/pad | solution.py:326
  84.7 11.2 %all-to-all-start = ((bf16[32,208,128]{2,1,0:T(8,128)(2,1)}), bf16[32,208,128]{2,1,0:T(8,128)(2,1)S(1)}, u32[]{:S(2)}, u32[]{:S(2)}) async-start(bf16[32,208,128]{2,1,0:T(8,128)(2,1)} %pad.4), calls=%async_computation | async-start | bytes 3407872 | tf_op jit(solution)/shard_map/all_to_all | solution.py:327
  95.9 0.8 constant_dynamic-slice_fusion.1
  96.7 0.8 copy.10
  97.5 0.0 copy-done
  97.5 0.8 copy.11
  98.2 0.6 fusion.w2t0
  98.8 36.4 %all-to-all-done.qkv = bf16[32,208,128]{2,1,0:T(8,128)(2,1)S(1)} async-done(((bf16[32,208,128]{2,1,0:T(8,128)(2,1)}), bf16[32,208,128]{2,1,0:T(8,128)(2,1)S(1)}, u32[]{:S(2)}, u32[]{:S(2)}) %all-to-all-start) | async-done | bytes 1703968 | tf_op jit(solution)/shard_map/all_to_all | solution.py:327
  135.2 0.0 copy-start.1
  135.2 1.2 copy-done.1
  136.4 38.6 %ttt_scan.1 = bf16[32,64,128]{2,1,0:T(8,128)(2,1)} custom-call(bf16[32,208,128]{2,1,0:T(8,128)(2,1)} %copy-done.1, f32[256,64]{1,0:T(8,128)} %bitcast.17, f32[64,256]{1,0:T(8,128)} %fusion.w2t0, f32[256,64]{1,0:T(8,128)} %bitcast.18), custom_call_target="tpu_custom_call" | custom-call | tf_op jit(solution)/shard_map/ttt_scan/pallas_call | solution.py:303
  175.0 22.9 %all_to_all.10 = bf16[32,64,128]{2,1,0:T(8,128)(2,1)S(1)} all-to-all(bf16[32,64,128]{2,1,0:T(8,128)(2,1)} %ttt_scan.1), channel_id=1, replica_groups=mesh['seg'=32,'head'=16] {'seg'}, dimensions={0} | all-to-all | bytes 1048576 | tf_op jit(solution)/shard_map/all_to_all | solution.py:332
  198.0 0.8 slice.4
  (1 shorter events, 0.0 us)
Async XLA Ops:
  0.0 97.5 %copy-start = (f32[3,64,256]{2,1,0:T(8,128)S(1)}, f32[3,64,256]{2,1,0:T(8,128)}, u32[]{:S(2)}) copy-start(f32[3,64,256]{2,1,0:T(8,128)} %param.14) | copy-start | bytes 589828
  84.7 50.5 %all-to-all-start = ((bf16[32,208,128]{2,1,0:T(8,128)(2,1)}), bf16[32,208,128]{2,1,0:T(8,128)(2,1)S(1)}, u32[]{:S(2)}, u32[]{:S(2)}) async-start(bf16[32,208,128]{2,1,0:T(8,128)(2,1)} %pad.4), calls=%async_computation | async-start | bytes 3407872 | tf_op jit(solution)/shard_map/all_to_all | solution.py:327
  135.2 1.2 copy-start.1

commit v3 on v2

--- a/solution.py
+++ b/solution.py
@@ -226,14 +226,15 @@
     return sq, t, half, hb, rs, y, y + (xt - st)
 
 
-def scan_items(get, put, w1t0, w2t0, w2c0, w1s, w2s, w2ts, ub, xs, rprev, count):
+def scan_items(get, put, ready, leave, w10, w2t0, w1s, w2s, w2ts, ub, xs, rprev, count):
     left = lax.broadcasted_iota(jnp.int32, (64, 128), 1) < 64
     left1 = lax.broadcasted_iota(jnp.int32, (1, 128), 1) < 64
     zero = jnp.zeros((64, 128), F32)
     zero1 = jnp.zeros((1, 128), F32)
-    w1s[...] = w1t0[...]
-    w2s[...] = w2t0[...]
-    w2ts[...] = w2c0[...]
+    w1s[...] = w10.T
+    w2s[...] = w2t0
+    w2ts[...] = w2t0.T
+    ready(0)
     x0 = jnp.where(left, get(0, 64, 64), zero)
     ub[...] = nn(w1s[...].astype(BF), x0.astype(BF))
     xs[...] = x0.T.astype(BF)
@@ -259,6 +260,11 @@
 
     def segment(s, carry):
         prev = jnp.maximum(s - 1, 0)
+
+        @pl.when(s + 1 < count)
+        def _():
+            ready(s + 1)
+
         qs, ks, vs = get(s, 0, 64), get(s, 64, 64), get(s, 128, 64)
         qp = get(prev, 0, 64)
         kn = get(jnp.minimum(s + 1, count - 1), 64, 64)
@@ -271,6 +277,11 @@
         rprev[...] = step(
             mid, jnp.where(left, zero, vs), jnp.where(left1, zero1, rate), jnp.where(left, kn, qs)
         )
+
+        @pl.when(s > 0)
+        def _():
+            leave(prev)
+
         return carry
 
     rprev[...] = zero
@@ -289,25 +300,170 @@
 ]
 
 
-def scan_kernel(qkv, w1t0, w2t0, w2c0, out, *scratch):
-    def get(s, row, rows):
-        return qkv[s, row : row + rows, :].astype(F32)
-
-    def put(s, value):
-        out[s] = value
-
-    scan_items(get, put, w1t0, w2t0, w2c0, *scratch, qkv.shape[0])
-
-
-def run_scan(qkv, w1t, w2t, w2c):
+def scan_kernel(items, w1, w2t, res, qkv, outs, isem, qsem, osem, rsem, *scratch):
+    me = lax.axis_index("seg")
+    barrier = pltpu.get_barrier_semaphore()
+
+    def greet(k, carry):
+        peer = lax.rem(me + k, 32)
+        pl.semaphore_signal(barrier, inc=1, device_id={"seg": peer}, device_id_type=MESH)
+        return carry
+
+    lax.fori_loop(1, 32, greet, 0)
+    pl.semaphore_wait(barrier, 31)
+
+    def item_out(i):
+        return pltpu.make_async_remote_copy(
+            src_ref=items.at[i],
+            dst_ref=qkv.at[me],
+            send_sem=isem.at[i],
+            recv_sem=qsem.at[me],
+            device_id={"seg": i},
+            device_id_type=MESH,
+        )
+
+    def item_in(s):
+        return pltpu.make_async_remote_copy(
+            src_ref=items.at[0],
+            dst_ref=qkv.at[s],
+            send_sem=isem.at[0],
+            recv_sem=qsem.at[s],
+            device_id={"seg": s},
+            device_id_type=MESH,
+        )
+
+    own = jnp.minimum(me, 23)
+    video, head = own // 3, lax.rem(own, 3)
+
+    def item_own():
+        return pltpu.make_async_copy(items.at[own], qkv.at[own], qsem.at[own])
+
+    def home(s):
+        return pltpu.make_async_remote_copy(
+            src_ref=outs.at[s],
+            dst_ref=res.at[video, pl.ds(pl.multiple_of(64 * head, 64), 64), :],
+            send_sem=osem.at[s],
+            recv_sem=rsem.at[own],
+            device_id={"seg": s},
+            device_id_type=MESH,
+        )
+
+    def home_own():
+        return pltpu.make_async_copy(
+            outs.at[own],
+            res.at[video, pl.ds(pl.multiple_of(64 * head, 64), 64), :],
+            rsem.at[own],
+        )
+
+    def home_in(i):
+        return pltpu.make_async_remote_copy(
+            src_ref=outs.at[0],
+            dst_ref=res.at[i // 3, pl.ds(pl.multiple_of(64 * lax.rem(i, 3), 64), 64), :],
+            send_sem=osem.at[0],
+            recv_sem=rsem.at[i],
+            device_id={"seg": i},
+            device_id_type=MESH,
+        )
+
+    @pl.when(me < 24)
+    def _():
+        item_own().start()
+
+    def send(k, carry):
+        i = lax.rem(me + k, 24)
+
+        @pl.when(i != me)
+        def _():
+            item_out(i).start()
+
+        return carry
+
+    lax.fori_loop(0, 24, send, 0)
+
+    def leave_home(s):
+        @pl.when(s == me)
+        def _():
+            home_own().start()
+
+        @pl.when(s != me)
+        def _():
+            home(s).start()
+
+    @pl.when(me < 24)
+    def _():
+        def get(s, row, rows):
+            return qkv[s, row : row + rows, :].astype(F32)
+
+        def put(s, value):
+            outs[s] = value
+
+        def ready(s):
+            @pl.when(s == me)
+            def _():
+                item_own().wait()
+
+            @pl.when(s != me)
+            def _():
+                item_in(s).wait_recv()
+
+        scan_items(get, put, ready, leave_home, w1[head], w2t[head], *scratch, 32)
+
+    def drain_sends(i, carry):
+        @pl.when(i != me)
+        def _():
+            item_out(i).wait_send()
+
+        return carry
+
+    lax.fori_loop(0, 24, drain_sends, 0)
+
+    @pl.when(me < 24)
+    def _():
+        leave_home(31)
+
+    def drain_items(i, carry):
+        @pl.when(i != me)
+        def _():
+            home_in(i).wait_recv()
+
+        @pl.when(i == me)
+        def _():
+            home_own().wait()
+
+        return carry
+
+    lax.fori_loop(0, 24, drain_items, 0)
+
+    @pl.when(me < 24)
+    def _():
+        def drain_homes(s, carry):
+            @pl.when(s != me)
+            def _():
+                home(s).wait_send()
+
+            return carry
+
+        lax.fori_loop(0, 32, drain_homes, 0)
+
+
+def run_scan(items, w1, w2t):
     return pl.pallas_call(
         scan_kernel,
-        out_shape=jax.ShapeDtypeStruct((qkv.shape[0], 64, 128), BF),
-        in_specs=[VMEM_SPEC] * 4,
+        out_shape=jax.ShapeDtypeStruct((8, 192, 128), BF),
+        in_specs=[VMEM_SPEC] * 3,
         out_specs=VMEM_SPEC,
-        scratch_shapes=SCAN_SCRATCH,
+        scratch_shapes=[
+            pltpu.VMEM((32, 208, 128), BF),
+            pltpu.VMEM((32, 64, 128), BF),
+            pltpu.SemaphoreType.DMA((24,)),
+            pltpu.SemaphoreType.DMA((32,)),
+            pltpu.SemaphoreType.DMA((32,)),
+            pltpu.SemaphoreType.DMA((24,)),
+        ]
+        + SCAN_SCRATCH,
+        compiler_params=pltpu.CompilerParams(collective_id=1, has_side_effects=True),
         name="ttt_scan",
-    )(qkv, w1t, w2t, w2c)
+    )(items, w1, w2t)
 
 
 def body(attn_query, attn_key, attn_value, prompt_len, ttt_weight, init_w1, init_w2t, step_rate):
@@ -322,16 +478,8 @@
         ttt_weight.T,
         jnp.swapaxes(step_rate, 0, 1),
     )
-    seg_count = lax.axis_size("seg")
-    items = jnp.pad(items, ((0, seg_count - items.shape[0]), (0, 0), (0, 0)))
-    sequence = lax.all_to_all(items, "seg", 0, 0, tiled=True)
-    head = lax.axis_index("seg") % 3
-    w1 = lax.dynamic_index_in_dim(init_w1, head, 0, keepdims=False)
-    w2t = lax.dynamic_index_in_dim(init_w2t, head, 0, keepdims=False)
-    outputs = run_scan(sequence, w1.T, w2t, w2t.T)
-    returned = lax.all_to_all(outputs, "seg", 0, 0, tiled=True)
-    returned = returned[:24].reshape(8, 192, 128)
-    return jnp.swapaxes(returned, 1, 2)
+    results = run_scan(items, init_w1, init_w2t)
+    return turned(results)
 
 
 def solution(mesh):

time: 199 us -> 157 us (0.79)
  the two profiles are of different devices: /device:TPU:1 before, /device:TPU:63 now
where the time goes in v3:
time: 157 us
  Pallas kernels  154 us (98%)
  local copies, waits for them, and re-layouts  3.09 us (2%)
    pallas_call x1, Pallas kernels, gather_project(): pl.pallas_call(gather_kernel, out_shape=jax.ShapeDtypeStruct((24, 208, 12...  82.9 us
    pallas_call x1, Pallas kernels, run_scan(): pl.pallas_call(scan_kernel, out_shape=jax.ShapeDtypeStruct((8, 192, 128),...  71.1 us

profile of v3, /device:TPU:63, one launch (start us, length us, event | category | flops | bytes accessed | tf_op | source)
XLA Modules:
  0.0 157.1 jit_solution(3815048992441247282)
XLA Ops:
  0.0 1.3 copy.9.lengths
  1.3 82.9 %attend_gather_project.1.items = bf16[24,208,128]{2,1,0:T(8,128)(2,1)} custom-call(s32[8,1]{1,0:T(8,128)} %copy.9.lengths, bf16[8,192,128]{2,1,0:T(8,128)(2,1)} %bitcast.8, bf16[8,192,128]{2,1,0:T(8,128)(2,1)} %bitcast.9, bf16[8,192,128]{2,1,0:T(8,128)(2,1)} %bitcast.10, bf16[576,3072]{1,0:T(8,128)(2,1)} %bitcast.6, f32[3,8,128]{2,1,0:T(8,128)} %bitcast.11), custom_call_target="tpu_custom_call" | custom-call | tf_op jit(solution)/shard_map/attend_gather_project/pallas_call | solution.py:187
  84.2 71.1 %ttt_scan.1 = bf16[8,192,128]{2,1,0:T(8,128)(2,1)} custom-call(bf16[24,208,128]{2,1,0:T(8,128)(2,1)} %attend_gather_project.1.items, f32[3,64,256]{2,1,0:T(8,128)} %w1.1, f32[3,64,256]{2,1,0:T(8,128)} %w2t.1), custom_call_target="tpu_custom_call" | custom-call | tf_op jit(solution)/shard_map/ttt_scan/pallas_call | solution.py:450
  155.4 1.8 %copy.11 = bf16[8,128,192]{1,2,0:T(8,128)(2,1)} copy(bf16[8,128,192]{1,2,0:T(8,128)(2,1)} %bitcast.7) | data formatting | bytes 786432

commit v4 on v3

v4 whole, which is shorter than its diff:
```python
import math

import jax
import jax.numpy as jnp
from jax import lax
from jax.experimental import pallas as pl
from jax.experimental.pallas import tpu as pltpu
from jax.sharding import PartitionSpec as P

F32, BF = jnp.float32, jnp.bfloat16
GC = math.sqrt(2.0 / math.pi)
GA = 0.044715
MESH = pl.DeviceIdType.MESH
VMEM_SPEC = pl.BlockSpec(memory_space=pltpu.VMEM)


def nn(a, b):
    return lax.dot_general(a, b, (((1,), (0,)), ((), ())), preferred_element_type=F32)


def nt(a, b):
    return lax.dot_general(a, b, (((1,), (1,)), ((), ())), preferred_element_type=F32)


def tn(a, b):
    return lax.dot_general(a, b, (((0,), (0,)), ((), ())), preferred_element_type=F32)


def attend(q, k, v, length, put):
    position = lax.broadcasted_iota(jnp.int32, (128, 1), 0)
    usable = (position >= 64) | (position < length)
    for h in range(3):
        rows = slice(64 * h, 64 * h + 64)
        scores = tn(k[rows, :], q[rows, :]) * 0.125
        scores = jnp.where(usable, scores, -1e30)
        exponent = jnp.exp(scores - jnp.max(scores, axis=0, keepdims=True))
        weights = (exponent * (1.0 / jnp.sum(exponent, axis=0, keepdims=True))).astype(BF)
        put(h, nn(v[rows, :], weights).astype(BF))


def item_of(video, group, head):
    return (video * 2 + group) * 3 + head


def gather_kernel(
    lengths, q, k, v, wt, rate, w1, w2t, out, wsel,
    buf, pbuf, acc, ssq, wv, wb, rate2,
    wsem, isem, psem, rsem, lsem, recv, usem, urecv, dsem, drecv, xrs, xls, msem, wrecv,
):
    me_h, me_s = lax.axis_index("head"), lax.axis_index("seg")
    z, y = me_h // 2, lax.rem(me_h, 2)
    row, x, core = me_s // 8, lax.rem(me_s // 2, 4), lax.rem(me_s, 2)
    other = 1 - y

    def device(seg, head):
        return {"seg": seg, "head": head}

    right, left = device(me_s, lax.rem(me_h + 2, 16)), device(me_s, lax.rem(me_h + 14, 16))
    partner = device(me_s, 2 * z + other)
    above = device(lax.rem(me_s + 8, 32), 2 * z + lax.rem(y + (row + 1) // 4, 2))
    below = device(lax.rem(me_s + 24, 32), 2 * z + lax.rem(y + (4 - row) // 4, 2))
    xup = device(8 * row + 2 * lax.rem(x + 1, 4) + core, me_h)
    xdown = device(8 * row + 2 * lax.rem(x + 3, 4) + core, me_h)
    mate = device(8 * row + 2 * x + 1 - core, me_h)
    barrier = pltpu.get_barrier_semaphore()
    for peer in (right, left, partner, above, below, xup, xdown, mate):
        pl.semaphore_signal(barrier, inc=1, device_id=peer, device_id_type=MESH)
    load = pltpu.make_async_copy(wt, wv, wsem)
    load.start()
    pl.semaphore_wait(barrier, 8)

    def remote(src, dst, send, receive, peer):
        return pltpu.make_async_remote_copy(
            src_ref=src, dst_ref=dst, send_sem=send, recv_sem=receive,
            device_id=peer, device_id_type=MESH,
        )

    item = jnp.minimum(me_s, 23)
    head, group = lax.rem(item, 3), lax.rem(item // 3, 2)

    def start_weight(n):
        source = w1 if n == 0 else w2t
        return remote(source.at[head], wsel.at[n], isem.at[2 + n], isem.at[n], partner)

    def start_local(n):
        source = w1 if n == 0 else w2t
        return pltpu.make_async_copy(source.at[head], wsel.at[n], isem.at[n])

    rates = remote(rate, rate2, isem.at[4], isem.at[5], partner)
    rates.start()

    @pl.when(group == y)
    def _():
        for n in range(2):
            start_local(n).start()
            start_weight(n).start()


    def block(zo, c, yo, sem, peer):
        return remote(buf.at[zo, c, yo], buf.at[zo, c, yo], sem, recv.at[zo, c, yo], peer)

    def to_right(zo, c, yo, d, o):
        return block(zo, c, yo, rsem.at[d, o, c], right)

    def to_left(zo, c, yo, d, o):
        return block(zo, c, yo, lsem.at[d, o, c], left)

    def to_partner(c):
        return remote(pbuf.at[c], buf.at[z, c, y], psem.at[c], recv.at[z, c, y], partner)

    zc = 2 * x + core

    def upper(n):
        return pl.ds(96 * n, 96)

    def lower(n):
        return pl.ds(288 + 96 * n, 96)

    lanes = pl.ds(pl.multiple_of(zc * 384, 128), 384)

    def up_first(n):
        return remote(wv.at[upper(n), lanes], wb.at[zc, upper(n), :], usem.at[n], urecv.at[n], above)

    def up_next(n):
        return remote(wb.at[zc, upper(n), :], wb.at[zc, upper(n), :], usem.at[n], urecv.at[n], above)

    def down_first(n):
        return remote(wv.at[lower(n), lanes], wb.at[zc, lower(n), :], dsem.at[n], drecv.at[n], below)

    def down_next(n):
        return remote(wb.at[zc, lower(n), :], wb.at[zc, lower(n), :], dsem.at[n], drecv.at[n], below)

    def weight(chunk, g, sem, peer):
        part = wb.at[chunk, pl.ds(288 * g, 288), :]
        return remote(part, part, sem, wrecv.at[chunk, g], peer)

    def to_mate(dx, g):
        return weight(2 * lax.rem(x + dx, 4) + core, g, msem.at[dx, g], mate)

    def attend_pair(pair, put_half):
        for half in range(2):
            video = 2 * pair + half

            def put(h, value):
                put_half(slice(64 * h, 64 * h + 64), slice(128 * half, 128 * half + 128), value)

            attend(q[video], k[video], v[video], lengths[video, 0], put)

    def attend_partner(c, carry):
        def put_half(rows, cols, value):
            pbuf[c, rows, cols] = value

        attend_pair(2 * other + c, put_half)

        @pl.when(c == 1)
        def _():
            to_partner(0).start()

        return carry

    lax.fori_loop(0, 2, attend_partner, 0)
    load.wait()

    @pl.when(row == 3)
    def _():
        for n in range(3):
            up_first(n).start()

    @pl.when(row == 0)
    def _():
        for n in range(3):
            down_first(n).start()

    def attend_own(c, carry):
        def put_half(rows, cols, value):
            buf[z, c, y, rows, cols] = value

        attend_pair(2 * y + c, put_half)

        @pl.when(c == 0)
        def _():
            to_partner(1).start()

        @pl.when(c == 1)
        def _():
            to_right(z, 0, y, 0, 0).start()
            to_left(z, 0, y, 0, 0).start()

        return carry

    lax.fori_loop(0, 2, attend_own, 0)

    def relay(n, carry):
        up_next(n).wait_recv()

        @pl.when(row < 3)
        def _():
            up_next(n).start()

        down_next(n).wait_recv()

        @pl.when(row > 0)
        def _():
            down_next(n).start()

        @pl.when(n < 2)
        def _():
            block(z, n, other, psem.at[n], partner).wait_recv()
            to_right(z, n, other, 0, 1).start()
            to_left(z, n, other, 0, 1).start()

        return carry

    acc[...] = jnp.zeros((2, 2, 576, 256), F32)
    ssq[...] = jnp.zeros((2, 8, 256), F32)
    to_right(z, 1, y, 0, 0).start()
    to_left(z, 1, y, 0, 0).start()
    lax.fori_loop(0, 3, relay, 0)
    for g in range(2):
        weight(zc, g, xrs.at[g], xup).start()
        weight(zc, g, xls.at[g], xdown).start()
        to_mate(0, g).start()

    def add(zo, c):
        xb = buf[zo, c].reshape(384, 256)
        w = wv[:, pl.ds(pl.multiple_of(zo * 384, 128), 384)]
        acc[0, c] += nn(w, xb)
        xf = xb.astype(F32)
        ssq[c] += jnp.sum((xf * xf).reshape(48, 8, 256), axis=0)

    def add_other(zo, c):
        acc[1, c] += nn(wb[zo], buf[zo, c].reshape(384, 256))

    def source(j, d):
        return lax.rem(z + 8 + (1 - 2 * (j // 2)) * d, 8)

    def hop(d, carry):
        zr, zl = lax.rem(z + 8 - d, 8), lax.rem(z + d, 8)
        for o in range(2):
            yo = y if o == 0 else other

            def chunk(c, inner):
                to_right(zr, c, yo, 0, 0).wait_recv()

                @pl.when((d < 3) | (c == 0))
                def _():
                    to_right(zr, c, yo, d, o).start()

                to_left(zl, c, yo, 0, 0).wait_recv()

                @pl.when((d < 3) | (c == 1))
                def _():
                    to_left(zl, c, yo, d, o).start()

                return inner

            lax.fori_loop(0, 2, chunk, 0)

        def add_hop(j, inner):
            add(source(j, d - 1), lax.rem(j, 2))
            return inner

        lax.fori_loop(0, jnp.minimum(2 * d, 4), add_hop, 0)

        @pl.when(d == 1)
        def _():
            behind, ahead = 2 * lax.rem(x + 3, 4) + core, 2 * lax.rem(x + 1, 4) + core
            weight(behind, 0, xrs.at[0], xup).wait_recv()
            weight(behind, 0, xrs.at[2], xup).start()
            weight(ahead, 1, xls.at[1], xdown).wait_recv()
            weight(ahead, 1, xls.at[2], xdown).start()
            to_mate(3, 0).start()
            to_mate(1, 1).start()
            weight(behind, 1, xrs.at[1], xup).wait_recv()
            to_mate(3, 1).start()
            weight(ahead, 0, xls.at[0], xdown).wait_recv()
            to_mate(1, 0).start()

        @pl.when(d == 2)
        def _():
            far = 2 * lax.rem(x + 2, 4) + core
            for g in range(2):
                weight(far, g, xrs.at[2], xup).wait_recv()
                to_mate(2, g).start()

        return carry

    lax.fori_loop(1, 4, hop, 0)

    def from_mate(n, carry):
        for g in range(2):
            weight(2 * n + 1 - core, g, msem.at[0, 0], mate).wait_recv()
        return carry

    lax.fori_loop(0, 4, from_mate, 0)

    def add_last(j, inner):
        add(source(j, 3), lax.rem(j, 2))
        return inner

    lax.fori_loop(0, 4, add_last, 0)

    def other_group(n, carry):
        add_other(lax.rem(z + 5 + n // 2, 8), lax.rem(n, 2))
        return carry

    lax.fori_loop(0, 14, other_group, 0)
    opposite = lax.rem(z + 4, 8)

    def final(c, carry):
        for o in range(2):
            yo = y if o == 0 else other

            @pl.when(c == 0)
            def _():
                to_right(opposite, c, yo, 0, 0).wait_recv()

            @pl.when(c == 1)
            def _():
                to_left(opposite, c, yo, 0, 0).wait_recv()

        add(opposite, c)
        add_other(opposite, c)
        return carry

    lax.fori_loop(0, 2, final, 0)
    rates.wait_recv()
    position = lax.broadcasted_iota(jnp.int32, (1, 128), 1)

    def finish(c, carry):
        mean = jnp.sum(ssq[c], axis=0, keepdims=True) * (1.0 / 3072.0)
        scale = lax.rsqrt(mean + 1e-6)
        for g in range(2):
            projected = (acc[g, c] * scale).astype(BF)
            source_rate = rate if g == 0 else rate2
            for half in range(2):
                video = 4 * y + 2 * c + half
                usable = (position >= 64) | (position < lengths[video, 0])
                for h in range(3):
                    slot = item_of(2 * c + half, y if g == 0 else other, h)
                    out[slot, 0:192, :] = projected[
                        192 * h : 192 * h + 192, 128 * half : 128 * half + 128
                    ]
                    eta = jnp.where(usable, source_rate[h, pl.ds(video, 1), :], 0.0)
                    out[slot, 192:208, :] = jnp.broadcast_to(eta, (16, 128)).astype(BF)
        return carry

    lax.fori_loop(0, 2, finish, 0)


    rates.wait_send()

    @pl.when(group == y)
    def _():
        for n in range(2):
            start_local(n).wait()
            start_weight(n).wait_send()

    @pl.when(group != y)
    def _():
        for n in range(2):
            start_weight(n).wait_recv()

    @pl.when(row < 3)
    def _():
        for n in range(3):
            up_next(n).wait_send()

    @pl.when(row == 3)
    def _():
        for n in range(3):
            up_first(n).wait_send()

    @pl.when(row > 0)
    def _():
        for n in range(3):
            down_next(n).wait_send()

    @pl.when(row == 0)
    def _():
        for n in range(3):
            down_first(n).wait_send()

    for n in range(3):
        weight(zc, 0, xrs.at[n], xup).wait_send()
        weight(zc, 0, xls.at[n], xdown).wait_send()
    for dx in range(4):
        for g in range(2):
            to_mate(dx, g).wait_send()

    def drain(c, carry):
        to_partner(c).wait_send()
        for o in range(2):
            for d in range(3):
                to_right(z, c, y, d, o).wait_send()
                to_left(z, c, y, d, o).wait_send()

            @pl.when(c == 0)
            def _():
                to_right(z, c, y, 3, o).wait_send()

            @pl.when(c == 1)
            def _():
                to_left(z, c, y, 3, o).wait_send()

        return carry

    lax.fori_loop(0, 2, drain, 0)


def gather_project(lengths, q, k, v, wt, rate, w1, w2t):
    any_spec = pl.BlockSpec(memory_space=pl.ANY)
    dma = pltpu.SemaphoreType.DMA
    return pl.pallas_call(
        gather_kernel,
        out_shape=(
            jax.ShapeDtypeStruct((24, 208, 128), BF),
            jax.ShapeDtypeStruct((2, 64, 256), F32),
        ),
        in_specs=[
            pl.BlockSpec(memory_space=pltpu.SMEM),
            VMEM_SPEC,
            VMEM_SPEC,
            VMEM_SPEC,
            any_spec,
            VMEM_SPEC,
            VMEM_SPEC,
            VMEM_SPEC,
        ],
        out_specs=(VMEM_SPEC, VMEM_SPEC),
        scratch_shapes=[
            pltpu.VMEM((8, 2, 2, 192, 256), BF),
            pltpu.VMEM((2, 192, 256), BF),
            pltpu.VMEM((2, 2, 576, 256), F32),
            pltpu.VMEM((2, 8, 256), F32),
            pltpu.VMEM((576, 3072), BF),
            pltpu.VMEM((8, 576, 384), BF),
            pltpu.VMEM((3, 8, 128), F32),
            dma,
            dma((6,)),
            dma((2,)),
            dma((4, 2, 2)),
            dma((4, 2, 2)),
            dma((8, 2, 2)),
            dma((3,)),
            dma((3,)),
            dma((3,)),
            dma((3,)),
            dma((3,)),
            dma((3,)),
            dma((4, 2)),
            dma((8, 2)),
        ],
        compiler_params=pltpu.CompilerParams(
            collective_id=0, has_side_effects=True, vmem_limit_bytes=56 << 20
        ),
        name="attend_gather_project",
    )(lengths, q, k, v, wt, rate, w1, w2t)


def forward(u, w2b, xt, st):
    sq = u * u
    t = jnp.tanh(u * (GC + (GC * GA) * sq))
    half = 0.5 + 0.5 * t
    hb = (u * half).astype(BF)
    z = nn(w2b, hb)
    center = z - jnp.mean(z, axis=0, keepdims=True)
    rs = lax.rsqrt(jnp.mean(center * center, axis=0, keepdims=True) + 1e-5)
    y = center * rs
    return sq, t, half, hb, rs, y, y + (xt - st)


def scan_items(get, put, ready, leave, w10, w2t0, w1s, w2s, w2ts, ub, xs, rprev, count):
    left = lax.broadcasted_iota(jnp.int32, (64, 128), 1) < 64
    left1 = lax.broadcasted_iota(jnp.int32, (1, 128), 1) < 64
    zero = jnp.zeros((64, 128), F32)
    zero1 = jnp.zeros((1, 128), F32)
    w1s[...] = w10.T
    w2s[...] = w2t0
    w2ts[...] = w2t0.T
    ready(0)
    x0 = jnp.where(left, get(0, 64, 64), zero)
    ub[...] = nn(w1s[...].astype(BF), x0.astype(BF))
    xs[...] = x0.T.astype(BF)

    def step(xt, st, eta, xnt):
        xntb = xnt.astype(BF)
        u = ub[...]
        sq, t, half, hb, rs, y, r = forward(u, w2s[...].astype(BF), xt, st)
        dy = r * (eta * (1.0 / 64.0))
        m1 = jnp.mean(dy, axis=0, keepdims=True)
        m2 = jnp.mean(dy * y, axis=0, keepdims=True)
        dzb = (rs * (dy - m1 - y * m2)).astype(BF)
        slope = half + (0.5 * u) * ((1.0 - t * t) * (GC + (3.0 * GC * GA) * sq))
        dub = (nn(w2ts[...].astype(BF), dzb) * slope).astype(BF)
        x = xs[...]
        w1 = w1s[...]
        ub[...] = nn(w1.astype(BF), xntb) - nn(dub, nn(x, xntb).astype(BF))
        w1s[...] = w1 - nn(dub, x)
        w2s[...] -= nt(dzb, hb)
        w2ts[...] -= nt(hb, dzb)
        xs[...] = xnt.T.astype(BF)
        return r

    def segment(s, carry):
        prev = jnp.maximum(s - 1, 0)

        @pl.when(s + 1 < count)
        def _():
            ready(s + 1)

        qs, ks, vs = get(s, 0, 64), get(s, 64, 64), get(s, 128, 64)
        qp = get(prev, 0, 64)
        kn = get(jnp.minimum(s + 1, count - 1), 64, 64)
        rate = get(s, 192, 1)
        mid = jnp.where(left, qs, ks)
        even = step(
            jnp.where(left, ks, qp), jnp.where(left, vs, zero), jnp.where(left1, rate, zero1), mid
        )
        put(prev, jnp.where(left, rprev[...], even).astype(BF))
        rprev[...] = step(
            mid, jnp.where(left, zero, vs), jnp.where(left1, zero1, rate), jnp.where(left, kn, qs)
        )

        @pl.when(s > 0)
        def _():
            leave(prev)

        return carry

    rprev[...] = zero
    lax.fori_loop(0, count, segment, 0)
    last = forward(ub[...], w2s[...].astype(BF), get(count - 1, 0, 64), zero)[-1]
    put(count - 1, jnp.where(left, rprev[...], last).astype(BF))


SCAN_SCRATCH = [
    pltpu.VMEM((256, 64), F32),
    pltpu.VMEM((64, 256), F32),
    pltpu.VMEM((256, 64), F32),
    pltpu.VMEM((256, 128), F32),
    pltpu.VMEM((128, 64), BF),
    pltpu.VMEM((64, 128), F32),
]


def scan_kernel(items, wsel, res, qkv, outs, isem, qsem, osem, rsem, *scratch):
    me, me_h = lax.axis_index("seg"), lax.axis_index("head")
    z, y = me_h // 2, lax.rem(me_h, 2)
    barrier = pltpu.get_barrier_semaphore()

    def greet(k, carry):
        peer = lax.rem(me + k, 32)
        pl.semaphore_signal(
            barrier, inc=1, device_id={"seg": peer, "head": me_h}, device_id_type=MESH
        )
        pl.semaphore_signal(
            barrier, inc=1, device_id={"seg": peer, "head": 2 * z + 1 - y}, device_id_type=MESH
        )
        return carry

    lax.fori_loop(1, 32, greet, 0)
    pl.semaphore_signal(
        barrier, inc=1, device_id={"seg": me, "head": 2 * z + 1 - y}, device_id_type=MESH
    )
    pl.semaphore_wait(barrier, 63)

    def item_out(i):
        return pltpu.make_async_remote_copy(
            src_ref=items.at[i],
            dst_ref=qkv.at[me],
            send_sem=isem.at[i],
            recv_sem=qsem.at[me],
            device_id={"seg": i, "head": me_h},
            device_id_type=MESH,
        )

    def item_in(s):
        return pltpu.make_async_remote_copy(
            src_ref=items.at[0],
            dst_ref=qkv.at[s],
            send_sem=isem.at[0],
            recv_sem=qsem.at[s],
            device_id={"seg": s, "head": me_h},
            device_id_type=MESH,
        )

    own = jnp.minimum(me, 23)
    video, group, head = 4 * y + own // 6, lax.rem(own // 3, 2), lax.rem(own, 3)

    def place(v, h):
        return res.at[v, pl.ds(pl.multiple_of(64 * h, 64), 64), :]

    def item_own():
        return pltpu.make_async_copy(items.at[own], qkv.at[own], qsem.at[own])

    def home(s):
        return pltpu.make_async_remote_copy(
            src_ref=outs.at[s],
            dst_ref=place(video, head),
            send_sem=osem.at[s],
            recv_sem=rsem.at[video * 3 + head],
            device_id={"seg": s, "head": 2 * z + group},
            device_id_type=MESH,
        )

    def home_own():
        return pltpu.make_async_copy(outs.at[own], place(video, head), rsem.at[video * 3 + head])

    def home_in(n):
        return pltpu.make_async_remote_copy(
            src_ref=outs.at[0],
            dst_ref=place(n // 3, lax.rem(n, 3)),
            send_sem=osem.at[0],
            recv_sem=rsem.at[n],
            device_id={"seg": me, "head": 2 * z + 1 - y},
            device_id_type=MESH,
        )

    def stays(s):
        return (s == me) & (group == y)

    @pl.when(me < 24)
    def _():
        item_own().start()

    def send(k, carry):
        i = lax.rem(me + k, 24)

        @pl.when(i != me)
        def _():
            item_out(i).start()

        return carry

    lax.fori_loop(0, 24, send, 0)

    def leave_home(s):
        @pl.when(stays(s))
        def _():
            home_own().start()

        @pl.when(jnp.logical_not(stays(s)))
        def _():
            home(s).start()

    @pl.when(me < 24)
    def _():
        def get(s, row, rows):
            return qkv[s, row : row + rows, :].astype(F32)

        def put(s, value):
            outs[s] = value

        def ready(s):
            @pl.when(s == me)
            def _():
                item_own().wait()

            @pl.when(s != me)
            def _():
                item_in(s).wait_recv()

        scan_items(get, put, ready, leave_home, wsel[0], wsel[1], *scratch, 32)

    def drain_sends(i, carry):
        @pl.when(i != me)
        def _():
            item_out(i).wait_send()

        return carry

    lax.fori_loop(0, 24, drain_sends, 0)

    @pl.when(me < 24)
    def _():
        leave_home(31)

    mine = (me < 24) & (group == y)

    def drain_items(n, carry):
        local = mine & (n == video * 3 + head)

        @pl.when(local)
        def _():
            home_own().wait()

        @pl.when(jnp.logical_not(local))
        def _():
            home_in(n).wait_recv()

        return carry

    lax.fori_loop(0, 24, drain_items, 0)

    @pl.when(me < 24)
    def _():
        def drain_homes(s, carry):
            @pl.when(jnp.logical_not(stays(s)))
            def _():
                home(s).wait_send()

            return carry

        lax.fori_loop(0, 32, drain_homes, 0)


def run_scan(items, wsel):
    return pl.pallas_call(
        scan_kernel,
        out_shape=jax.ShapeDtypeStruct((8, 192, 128), BF),
        in_specs=[VMEM_SPEC] * 2,
        out_specs=VMEM_SPEC,
        scratch_shapes=[
            pltpu.VMEM((32, 208, 128), BF),
            pltpu.VMEM((32, 64, 128), BF),
            pltpu.SemaphoreType.DMA((24,)),
            pltpu.SemaphoreType.DMA((32,)),
            pltpu.SemaphoreType.DMA((32,)),
            pltpu.SemaphoreType.DMA((24,)),
        ]
        + SCAN_SCRATCH,
        compiler_params=pltpu.CompilerParams(collective_id=1, has_side_effects=True),
        name="ttt_scan",
    )(items, wsel)


def body(attn_query, attn_key, attn_value, prompt_len, ttt_weight, init_w1, init_w2t, step_rate):
    def turned(array):
        return jnp.swapaxes(array, 1, 2)

    items, wsel = gather_project(
        prompt_len,
        turned(attn_query),
        turned(attn_key),
        turned(attn_value),
        ttt_weight.T,
        jnp.swapaxes(step_rate, 0, 1),
        init_w1,
        init_w2t,
    )
    results = run_scan(items, wsel)
    return turned(results)


def solution(mesh):
    in_specs = (
        P(None, "seg", "head"),
        P(None, "seg", "head"),
        P(None, "seg", "head"),
        P(None, "seg"),
        P(None, "head"),
        P("head", None, None),
        P("head", None, None),
        P(None, "head", "seg"),
    )
    return jax.shard_map(
        body, mesh=mesh, in_specs=in_specs, out_specs=P(None, "seg", "head"), check_vma=False
    )
```

time: 157 us -> 193 us (1.23)
  Pallas kernels: 154 us -> 190 us
    pallas_call x1, Pallas kernels: 71.1 us -> 89.3 us  [run_scan(): pl.pallas_call(scan_kernel, out_shape=jax.ShapeDtypeStruct((8, 192, 128),...]
    pallas_call x1, Pallas kernels: 82.9 us -> 101 us  [gather_project(): pl.pallas_call(gather_kernel, out_shape=(jax.ShapeDtypeStruct((24, 208, 1...]
where the time goes in v4:
time: 193 us
  Pallas kernels  190 us (98%)
  local copies, waits for them, and re-layouts  3.09 us (2%)
    pallas_call x1, Pallas kernels, gather_project(): pl.pallas_call(gather_kernel, out_shape=(jax.ShapeDtypeStruct((24, 208, 1...  101 us
    pallas_call x1, Pallas kernels, run_scan(): pl.pallas_call(scan_kernel, out_shape=jax.ShapeDtypeStruct((8, 192, 128),...  89.3 us

profile of v4, /device:TPU:63, one launch (start us, length us, event | category | flops | bytes accessed | tf_op | source)
XLA Modules:
  0.0 193.0 jit_solution(4209089504241417214)
XLA Ops:
  0.0 1.3 copy.9.lengths
  1.3 100.7 %attend_gather_project.1 = (bf16[24,208,128]{2,1,0:T(8,128)(2,1)}, f32[2,64,256]{2,1,0:T(8,128)}) custom-call(s32[8,1]{1,0:T(8,128)} %copy.9.lengths, bf16[8,192,128]{2,1,0:T(8,128)(2,1)} %bitcast.8, bf16[8,192,128]{2,1,0:T(8,128)(2,1)} %bitcast.9, bf16[8,192,128]{2,1,0:T(8,128)(2,1)} %bitcast.10, bf16[576,3072]{1,0:T(8,128)(2,1)} %bitcast.6, ...), custom_call_target="tpu_custom_call" | custom-call | tf_op jit(solution)/shard_map/attend_gather_project/pallas_call | solution.py:414
  102.0 89.3 %ttt_scan.1 = bf16[8,192,128]{2,1,0:T(8,128)(2,1)} custom-call(bf16[24,208,128]{2,1,0:T(8,128)(2,1)} %get-tuple-element.7.items, f32[2,64,256]{2,1,0:T(8,128)} %get-tuple-element.8.wsel), custom_call_target="tpu_custom_call" | custom-call | tf_op jit(solution)/shard_map/ttt_scan/pallas_call | solution.py:709
  191.3 1.8 copy.11

commit v5 on v4

--- a/solution.py
+++ b/solution.py
@@ -45,7 +45,7 @@
 def gather_kernel(
     lengths, q, k, v, wt, rate, w1, w2t, out, wsel,
     buf, pbuf, acc, ssq, wv, wb, rate2,
-    wsem, isem, psem, rsem, lsem, recv, usem, urecv, dsem, drecv, xrs, xls, msem, wrecv,
+    wsem, isem, psem, rsem, lsem, recv, csem, ysend, yrecv, xsem, msem, wrecv,
 ):
     me_h, me_s = lax.axis_index("head"), lax.axis_index("seg")
     z, y = me_h // 2, lax.rem(me_h, 2)
@@ -59,15 +59,14 @@
     partner = device(me_s, 2 * z + other)
     above = device(lax.rem(me_s + 8, 32), 2 * z + lax.rem(y + (row + 1) // 4, 2))
     below = device(lax.rem(me_s + 24, 32), 2 * z + lax.rem(y + (4 - row) // 4, 2))
-    xup = device(8 * row + 2 * lax.rem(x + 1, 4) + core, me_h)
-    xdown = device(8 * row + 2 * lax.rem(x + 3, 4) + core, me_h)
+    xpeer = [device(8 * row + 2 * lax.rem(x + dx, 4) + core, me_h) for dx in (1, 2, 3)]
     mate = device(8 * row + 2 * x + 1 - core, me_h)
     barrier = pltpu.get_barrier_semaphore()
-    for peer in (right, left, partner, above, below, xup, xdown, mate):
+    for peer in (right, left, partner, above, below, mate, *xpeer):
         pl.semaphore_signal(barrier, inc=1, device_id=peer, device_id_type=MESH)
     load = pltpu.make_async_copy(wt, wv, wsem)
     load.start()
-    pl.semaphore_wait(barrier, 8)
+    pl.semaphore_wait(barrier, 9)
 
     def remote(src, dst, send, receive, peer):
         return pltpu.make_async_remote_copy(
@@ -109,33 +108,36 @@
         return remote(pbuf.at[c], buf.at[z, c, y], psem.at[c], recv.at[z, c, y], partner)
 
     zc = 2 * x + core
-
-    def upper(n):
-        return pl.ds(96 * n, 96)
-
-    def lower(n):
-        return pl.ds(288 + 96 * n, 96)
-
     lanes = pl.ds(pl.multiple_of(zc * 384, 128), 384)
 
-    def up_first(n):
-        return remote(wv.at[upper(n), lanes], wb.at[zc, upper(n), :], usem.at[n], urecv.at[n], above)
-
-    def up_next(n):
-        return remote(wb.at[zc, upper(n), :], wb.at[zc, upper(n), :], usem.at[n], urecv.at[n], above)
-
-    def down_first(n):
-        return remote(wv.at[lower(n), lanes], wb.at[zc, lower(n), :], dsem.at[n], drecv.at[n], below)
-
-    def down_next(n):
-        return remote(wb.at[zc, lower(n), :], wb.at[zc, lower(n), :], dsem.at[n], drecv.at[n], below)
+    def half_of(chunk, g):
+        return wb.at[chunk, pl.ds(pl.multiple_of(288 * g, 32), 288), :]
+
+    def cross(g, peer):
+        source = wv.at[pl.ds(288 * g, 288), lanes]
+        return remote(source, half_of(zc, g), csem, yrecv.at[g], peer)
+
+    def onward(g):
+        peer = device(lax.rem(me_s + 8 + 16 * g, 32), me_h)
+        return remote(half_of(zc, g), half_of(zc, g), ysend.at[g], yrecv.at[g], peer)
 
     def weight(chunk, g, sem, peer):
-        part = wb.at[chunk, pl.ds(288 * g, 288), :]
-        return remote(part, part, sem, wrecv.at[chunk, g], peer)
+        return remote(half_of(chunk, g), half_of(chunk, g), sem, wrecv.at[chunk, g], peer)
+
+    def chunk_at(dx):
+        return 2 * lax.rem(x + dx, 4) + core
 
     def to_mate(dx, g):
-        return weight(2 * lax.rem(x + dx, 4) + core, g, msem.at[dx, g], mate)
+        return weight(chunk_at(dx), g, msem.at[dx, g], mate)
+
+    def spread(g):
+        for dx in (1, 3, 2):
+            weight(zc, g, xsem.at[dx - 1, g], xpeer[dx - 1]).start()
+        to_mate(0, g).start()
+
+    sooner = row // 2
+    later = 1 - sooner
+    edge = (row == 0) | (row == 3)
 
     def attend_pair(pair, put_half):
         for half in range(2):
@@ -146,12 +148,57 @@
 
             attend(q[video], k[video], v[video], lengths[video, 0], put)
 
+    def hop(d, o):
+        yo = y if o == 0 else other
+        zr, zl = lax.rem(z + 8 - d, 8), lax.rem(z + d, 8)
+        for c in range(2):
+            if d < 4 or c == 0:
+                to_right(zr, c, yo, 0, 0).wait_recv()
+            if d < 3 or (d == 3 and c == 0):
+                to_right(zr, c, yo, d, o).start()
+            if d < 4 or c == 1:
+                to_left(zl, c, yo, 0, 0).wait_recv()
+            if d < 3 or (d == 3 and c == 1):
+                to_left(zl, c, yo, d, o).start()
+
+    def attend_own(c, carry):
+        def put_half(rows, cols, value):
+            buf[z, c, y, rows, cols] = value
+
+        attend_pair(2 * y + c, put_half)
+
+        @pl.when(c == 0)
+        def _():
+            load.wait()
+
+            @pl.when(row == 3)
+            def _():
+                cross(0, above).start()
+
+            @pl.when(row == 0)
+            def _():
+                cross(1, below).start()
+
+        @pl.when(c == 1)
+        def _():
+            to_right(z, 0, y, 0, 0).start()
+            to_left(z, 0, y, 0, 0).start()
+
+        return carry
+
+    lax.fori_loop(0, 2, attend_own, 0)
+
     def attend_partner(c, carry):
         def put_half(rows, cols, value):
             pbuf[c, rows, cols] = value
 
         attend_pair(2 * other + c, put_half)
 
+        @pl.when(c == 0)
+        def _():
+            to_right(z, 1, y, 0, 0).start()
+            to_left(z, 1, y, 0, 0).start()
+
         @pl.when(c == 1)
         def _():
             to_partner(0).start()
@@ -159,171 +206,79 @@
         return carry
 
     lax.fori_loop(0, 2, attend_partner, 0)
-    load.wait()
-
-    @pl.when(row == 3)
-    def _():
-        for n in range(3):
-            up_first(n).start()
-
-    @pl.when(row == 0)
-    def _():
-        for n in range(3):
-            down_first(n).start()
-
-    def attend_own(c, carry):
-        def put_half(rows, cols, value):
-            buf[z, c, y, rows, cols] = value
-
-        attend_pair(2 * y + c, put_half)
-
-        @pl.when(c == 0)
-        def _():
-            to_partner(1).start()
-
-        @pl.when(c == 1)
-        def _():
-            to_right(z, 0, y, 0, 0).start()
-            to_left(z, 0, y, 0, 0).start()
-
-        return carry
-
-    lax.fori_loop(0, 2, attend_own, 0)
-
-    def relay(n, carry):
-        up_next(n).wait_recv()
-
-        @pl.when(row < 3)
-        def _():
-            up_next(n).start()
-
-        down_next(n).wait_recv()
-
-        @pl.when(row > 0)
-        def _():
-            down_next(n).start()
-
-        @pl.when(n < 2)
-        def _():
-            block(z, n, other, psem.at[n], partner).wait_recv()
-            to_right(z, n, other, 0, 1).start()
-            to_left(z, n, other, 0, 1).start()
-
-        return carry
-
     acc[...] = jnp.zeros((2, 2, 576, 256), F32)
     ssq[...] = jnp.zeros((2, 8, 256), F32)
-    to_right(z, 1, y, 0, 0).start()
-    to_left(z, 1, y, 0, 0).start()
-    lax.fori_loop(0, 3, relay, 0)
-    for g in range(2):
-        weight(zc, g, xrs.at[g], xup).start()
-        weight(zc, g, xls.at[g], xdown).start()
-        to_mate(0, g).start()
-
-    def add(zo, c):
+    to_partner(1).start()
+
+    @pl.when(edge)
+    def _():
+        onward(sooner).wait_recv()
+        onward(sooner).start()
+        spread(sooner)
+
+    hop(1, 0)
+
+    @pl.when(jnp.logical_not(edge))
+    def _():
+        onward(sooner).wait_recv()
+        onward(sooner).start()
+        spread(sooner)
+
+    for c in range(2):
+        block(z, c, other, psem.at[c], partner).wait_recv()
+        to_right(z, c, other, 0, 1).start()
+        to_left(z, c, other, 0, 1).start()
+    hop(2, 0)
+
+    @pl.when(jnp.logical_not(edge))
+    def _():
+        onward(later).wait_recv()
+        onward(later).start()
+        spread(later)
+
+    hop(1, 1)
+    hop(3, 0)
+
+    @pl.when(edge)
+    def _():
+        onward(later).wait_recv()
+        spread(later)
+
+    hop(2, 1)
+    for dx in (1, 3, 2):
+        weight(chunk_at(dx), sooner, csem, mate).wait_recv()
+        to_mate(dx, sooner).start()
+    hop(3, 1)
+
+    def add(n, carry):
+        zo, c = lax.rem(z + 5 + n // 2, 8), lax.rem(n, 2)
         xb = buf[zo, c].reshape(384, 256)
         w = wv[:, pl.ds(pl.multiple_of(zo * 384, 128), 384)]
         acc[0, c] += nn(w, xb)
         xf = xb.astype(F32)
         ssq[c] += jnp.sum((xf * xf).reshape(48, 8, 256), axis=0)
-
-    def add_other(zo, c):
+        return carry
+
+    lax.fori_loop(0, 14, add, 0)
+    hop(4, 0)
+    hop(4, 1)
+    lax.fori_loop(14, 16, add, 0)
+    for dx in (1, 3, 2):
+        weight(chunk_at(dx), later, csem, mate).wait_recv()
+        to_mate(dx, later).start()
+
+    def add_other(n, carry):
+        zo, c = 2 * lax.rem(n // 2, 4) + lax.rem(core + n // 8, 2), lax.rem(n, 2)
+
+        @pl.when((n >= 8) & (c == 0))
+        def _():
+            for g in range(2):
+                weight(zo, g, csem, mate).wait_recv()
+
         acc[1, c] += nn(wb[zo], buf[zo, c].reshape(384, 256))
-
-    def source(j, d):
-        return lax.rem(z + 8 + (1 - 2 * (j // 2)) * d, 8)
-
-    def hop(d, carry):
-        zr, zl = lax.rem(z + 8 - d, 8), lax.rem(z + d, 8)
-        for o in range(2):
-            yo = y if o == 0 else other
-
-            def chunk(c, inner):
-                to_right(zr, c, yo, 0, 0).wait_recv()
-
-                @pl.when((d < 3) | (c == 0))
-                def _():
-                    to_right(zr, c, yo, d, o).start()
-
-                to_left(zl, c, yo, 0, 0).wait_recv()
-
-                @pl.when((d < 3) | (c == 1))
-                def _():
-                    to_left(zl, c, yo, d, o).start()
-
-                return inner
-
-            lax.fori_loop(0, 2, chunk, 0)
-
-        def add_hop(j, inner):
-            add(source(j, d - 1), lax.rem(j, 2))
-            return inner
-
-        lax.fori_loop(0, jnp.minimum(2 * d, 4), add_hop, 0)
-
-        @pl.when(d == 1)
-        def _():
-            behind, ahead = 2 * lax.rem(x + 3, 4) + core, 2 * lax.rem(x + 1, 4) + core
-            weight(behind, 0, xrs.at[0], xup).wait_recv()
-            weight(behind, 0, xrs.at[2], xup).start()
-            weight(ahead, 1, xls.at[1], xdown).wait_recv()
-            weight(ahead, 1, xls.at[2], xdown).start()
-            to_mate(3, 0).start()
-            to_mate(1, 1).start()
-            weight(behind, 1, xrs.at[1], xup).wait_recv()
-            to_mate(3, 1).start()
-            weight(ahead, 0, xls.at[0], xdown).wait_recv()
-            to_mate(1, 0).start()
-
-        @pl.when(d == 2)
-        def _():
-            far = 2 * lax.rem(x + 2, 4) + core
-            for g in range(2):
-                weight(far, g, xrs.at[2], xup).wait_recv()
-                to_mate(2, g).start()
-
-        return carry
-
-    lax.fori_loop(1, 4, hop, 0)
-
-    def from_mate(n, carry):
-        for g in range(2):
-            weight(2 * n + 1 - core, g, msem.at[0, 0], mate).wait_recv()
-        return carry
-
-    lax.fori_loop(0, 4, from_mate, 0)
-
-    def add_last(j, inner):
-        add(source(j, 3), lax.rem(j, 2))
-        return inner
-
-    lax.fori_loop(0, 4, add_last, 0)
-
-    def other_group(n, carry):
-        add_other(lax.rem(z + 5 + n // 2, 8), lax.rem(n, 2))
-        return carry
-
-    lax.fori_loop(0, 14, other_group, 0)
-    opposite = lax.rem(z + 4, 8)
-
-    def final(c, carry):
-        for o in range(2):
-            yo = y if o == 0 else other
-
-            @pl.when(c == 0)
-            def _():
-                to_right(opposite, c, yo, 0, 0).wait_recv()
-
-            @pl.when(c == 1)
-            def _():
-                to_left(opposite, c, yo, 0, 0).wait_recv()
-
-        add(opposite, c)
-        add_other(opposite, c)
-        return carry
-
-    lax.fori_loop(0, 2, final, 0)
+        return carry
+
+    lax.fori_loop(0, 16, add_other, 0)
     rates.wait_recv()
     position = lax.broadcasted_iota(jnp.int32, (1, 128), 1)
 
@@ -361,32 +316,21 @@
         for n in range(2):
             start_weight(n).wait_recv()
 
-    @pl.when(row < 3)
-    def _():
-        for n in range(3):
-            up_next(n).wait_send()
-
-    @pl.when(row == 3)
-    def _():
-        for n in range(3):
-            up_first(n).wait_send()
-
-    @pl.when(row > 0)
-    def _():
-        for n in range(3):
-            down_next(n).wait_send()
-
-    @pl.when(row == 0)
-    def _():
-        for n in range(3):
-            down_first(n).wait_send()
-
-    for n in range(3):
-        weight(zc, 0, xrs.at[n], xup).wait_send()
-        weight(zc, 0, xls.at[n], xdown).wait_send()
-    for dx in range(4):
-        for g in range(2):
+    @pl.when(edge)
+    def _():
+        cross(0, above).wait_send()
+
+    onward(sooner).wait_send()
+
+    @pl.when(jnp.logical_not(edge))
+    def _():
+        onward(later).wait_send()
+
+    for g in range(2):
+        for dx in range(4):
             to_mate(dx, g).wait_send()
+        for dx in range(3):
+            weight(zc, g, xsem.at[dx, g], xpeer[dx]).wait_send()
 
     def drain(c, carry):
         to_partner(c).wait_send()
@@ -442,12 +386,10 @@
             dma((4, 2, 2)),
             dma((4, 2, 2)),
             dma((8, 2, 2)),
-            dma((3,)),
-            dma((3,)),
-            dma((3,)),
-            dma((3,)),
-            dma((3,)),
-            dma((3,)),
+            dma,
+            dma((2,)),
+            dma((2,)),
+            dma((3, 2)),
             dma((4, 2)),
             dma((8, 2)),
         ],

time: 193 us -> 153 us (0.79)
  Pallas kernels: 190 us -> 149 us
    pallas_call x1, Pallas kernels: 101 us -> 68.8 us  [gather_project(): pl.pallas_call(gather_kernel, out_shape=(jax.ShapeDtypeStruct((24, 208, 1...]
    pallas_call x1, Pallas kernels: 89.3 us -> 80.4 us  [run_scan(): pl.pallas_call(scan_kernel, out_shape=jax.ShapeDtypeStruct((8, 192, 128),...]
where the time goes in v5:
time: 153 us; the launch traced here: 152 us
  Pallas kernels  149 us (97%)
  local copies, waits for them, and re-layouts  3.09 us (2%)
    pallas_call x1, Pallas kernels, run_scan(): pl.pallas_call(scan_kernel, out_shape=jax.ShapeDtypeStruct((8, 192, 128),...  80.4 us
    pallas_call x1, Pallas kernels, gather_project(): pl.pallas_call(gather_kernel, out_shape=(jax.ShapeDtypeStruct((24, 208, 1...  68.8 us
    unnamed x2, local copies, waits for them, and re-layouts  3.09 us

profile of v5, /device:TPU:63, one launch (start us, length us, event | category | flops | bytes accessed | tf_op | source)
XLA Modules:
  0.0 152.3 jit_solution(1845457854496215179)
XLA Ops:
  0.0 1.3 copy.9.lengths
  1.3 68.8 %attend_gather_project.1 = (bf16[24,208,128]{2,1,0:T(8,128)(2,1)}, f32[2,64,256]{2,1,0:T(8,128)}) custom-call(s32[8,1]{1,0:T(8,128)} %copy.9.lengths, bf16[8,192,128]{2,1,0:T(8,128)(2,1)} %bitcast.8, bf16[8,192,128]{2,1,0:T(8,128)(2,1)} %bitcast.9, bf16[8,192,128]{2,1,0:T(8,128)(2,1)} %bitcast.10, bf16[576,3072]{1,0:T(8,128)(2,1)} %bitcast.6, ...), custom_call_target="tpu_custom_call" | custom-call | tf_op jit(solution)/shard_map/attend_gather_project/pallas_call | solution.py:358
  70.1 80.4 %ttt_scan.1 = bf16[8,192,128]{2,1,0:T(8,128)(2,1)} custom-call(bf16[24,208,128]{2,1,0:T(8,128)(2,1)} %get-tuple-element.7.items, f32[2,64,256]{2,1,0:T(8,128)} %get-tuple-element.8.wsel), custom_call_target="tpu_custom_call" | custom-call | tf_op jit(solution)/shard_map/ttt_scan/pallas_call | solution.py:651
  150.5 1.8 %copy.11 = bf16[8,128,192]{1,2,0:T(8,128)(2,1)} copy(bf16[8,128,192]{1,2,0:T(8,128)(2,1)} %bitcast.7) | data formatting | bytes 786432

commit v6 on v5

--- a/solution.py
+++ b/solution.py
@@ -96,7 +96,7 @@
 
 
     def block(zo, c, yo, sem, peer):
-        return remote(buf.at[zo, c, yo], buf.at[zo, c, yo], sem, recv.at[zo, c, yo], peer)
+        return remote(buf.at[c, zo, yo], buf.at[c, zo, yo], sem, recv.at[zo, c, yo], peer)
 
     def to_right(zo, c, yo, d, o):
         return block(zo, c, yo, rsem.at[d, o, c], right)
@@ -105,16 +105,17 @@
         return block(zo, c, yo, lsem.at[d, o, c], left)
 
     def to_partner(c):
-        return remote(pbuf.at[c], buf.at[z, c, y], psem.at[c], recv.at[z, c, y], partner)
+        return remote(pbuf.at[c], buf.at[c, z, y], psem.at[c], recv.at[z, c, y], partner)
 
     zc = 2 * x + core
     lanes = pl.ds(pl.multiple_of(zc * 384, 128), 384)
 
     def half_of(chunk, g):
-        return wb.at[chunk, pl.ds(pl.multiple_of(288 * g, 32), 288), :]
+        columns = pl.ds(pl.multiple_of(chunk * 384, 128), 384)
+        return wb.at[pl.ds(pl.multiple_of(288 * g, 32), 288), columns]
 
     def cross(g, peer):
-        source = wv.at[pl.ds(288 * g, 288), lanes]
+        source = wt.at[pl.ds(288 * g, 288), lanes]
         return remote(source, half_of(zc, g), csem, yrecv.at[g], peer)
 
     def onward(g):
@@ -146,47 +147,36 @@
             def put(h, value):
                 put_half(slice(64 * h, 64 * h + 64), slice(128 * half, 128 * half + 128), value)
 
-            attend(q[video], k[video], v[video], lengths[video, 0], put)
-
-    def hop(d, o):
+            attend(q[video], k[video], v[video], lengths[0, video], put)
+
+    def hop(d, o, c):
         yo = y if o == 0 else other
         zr, zl = lax.rem(z + 8 - d, 8), lax.rem(z + d, 8)
-        for c in range(2):
-            if d < 4 or c == 0:
-                to_right(zr, c, yo, 0, 0).wait_recv()
-            if d < 3 or (d == 3 and c == 0):
-                to_right(zr, c, yo, d, o).start()
-            if d < 4 or c == 1:
-                to_left(zl, c, yo, 0, 0).wait_recv()
-            if d < 3 or (d == 3 and c == 1):
-                to_left(zl, c, yo, d, o).start()
-
-    def attend_own(c, carry):
-        def put_half(rows, cols, value):
-            buf[z, c, y, rows, cols] = value
-
-        attend_pair(2 * y + c, put_half)
-
-        @pl.when(c == 0)
-        def _():
-            load.wait()
-
-            @pl.when(row == 3)
-            def _():
-                cross(0, above).start()
-
-            @pl.when(row == 0)
-            def _():
-                cross(1, below).start()
-
-        @pl.when(c == 1)
-        def _():
-            to_right(z, 0, y, 0, 0).start()
-            to_left(z, 0, y, 0, 0).start()
-
-        return carry
-
-    lax.fori_loop(0, 2, attend_own, 0)
+        if d < 4 or c == 0:
+            to_right(zr, c, yo, 0, 0).wait_recv()
+        if d < 3 or (d == 3 and c == 0):
+            to_right(zr, c, yo, d, o).start()
+        if d < 4 or c == 1:
+            to_left(zl, c, yo, 0, 0).wait_recv()
+        if d < 3 or (d == 3 and c == 1):
+            to_left(zl, c, yo, d, o).start()
+
+    def send_own(c):
+        to_right(z, c, y, 0, 0).start()
+        to_left(z, c, y, 0, 0).start()
+
+    def take_partner(c):
+        block(z, c, other, psem.at[c], partner).wait_recv()
+        to_right(z, c, other, 0, 1).start()
+        to_left(z, c, other, 0, 1).start()
+
+    @pl.when(row == 3)
+    def _():
+        cross(0, above).start()
+
+    @pl.when(row == 0)
+    def _():
+        cross(1, below).start()
 
     def attend_partner(c, carry):
         def put_half(rows, cols, value):
@@ -194,41 +184,52 @@
 
         attend_pair(2 * other + c, put_half)
 
+        @pl.when(c == 1)
+        def _():
+            to_partner(0).start()
+
+        return carry
+
+    lax.fori_loop(0, 2, attend_partner, 0)
+
+    def attend_own(c, carry):
+        def put_half(rows, cols, value):
+            buf[c, z, y, rows, cols] = value
+
+        attend_pair(2 * y + c, put_half)
+
         @pl.when(c == 0)
         def _():
-            to_right(z, 1, y, 0, 0).start()
-            to_left(z, 1, y, 0, 0).start()
+            to_partner(1).start()
+
+            @pl.when(edge)
+            def _():
+                onward(sooner).wait_recv()
+                onward(sooner).start()
+                spread(sooner)
 
         @pl.when(c == 1)
         def _():
-            to_partner(0).start()
-
-        return carry
-
-    lax.fori_loop(0, 2, attend_partner, 0)
+            send_own(0)
+
+        return carry
+
+    lax.fori_loop(0, 2, attend_own, 0)
+    load.wait()
     acc[...] = jnp.zeros((2, 2, 576, 256), F32)
-    ssq[...] = jnp.zeros((2, 8, 256), F32)
-    to_partner(1).start()
-
-    @pl.when(edge)
+    send_own(1)
+    hop(1, 0, 0)
+    hop(1, 0, 1)
+
+    @pl.when(jnp.logical_not(edge))
     def _():
         onward(sooner).wait_recv()
         onward(sooner).start()
         spread(sooner)
 
-    hop(1, 0)
-
-    @pl.when(jnp.logical_not(edge))
-    def _():
-        onward(sooner).wait_recv()
-        onward(sooner).start()
-        spread(sooner)
-
-    for c in range(2):
-        block(z, c, other, psem.at[c], partner).wait_recv()
-        to_right(z, c, other, 0, 1).start()
-        to_left(z, c, other, 0, 1).start()
-    hop(2, 0)
+    hop(2, 0, 0)
+    take_partner(0)
+    hop(2, 0, 1)
 
     @pl.when(jnp.logical_not(edge))
     def _():
@@ -236,49 +237,49 @@
         onward(later).start()
         spread(later)
 
-    hop(1, 1)
-    hop(3, 0)
+    hop(3, 0, 0)
+    hop(1, 1, 0)
+    hop(3, 0, 1)
+    take_partner(1)
+    hop(2, 1, 0)
 
     @pl.when(edge)
     def _():
         onward(later).wait_recv()
         spread(later)
 
-    hop(2, 1)
+    hop(1, 1, 1)
     for dx in (1, 3, 2):
         weight(chunk_at(dx), sooner, csem, mate).wait_recv()
         to_mate(dx, sooner).start()
-    hop(3, 1)
-
-    def add(n, carry):
-        zo, c = lax.rem(z + 5 + n // 2, 8), lax.rem(n, 2)
-        xb = buf[zo, c].reshape(384, 256)
-        w = wv[:, pl.ds(pl.multiple_of(zo * 384, 128), 384)]
-        acc[0, c] += nn(w, xb)
+    hop(3, 1, 0)
+    hop(2, 1, 1)
+    hop(4, 0, 0)
+    hop(4, 1, 0)
+
+    def project_own(c):
+        xb = buf[c].reshape(3072, 256)
+        acc[0, c] = nn(wv[...], xb)
         xf = xb.astype(F32)
-        ssq[c] += jnp.sum((xf * xf).reshape(48, 8, 256), axis=0)
-        return carry
-
-    lax.fori_loop(0, 14, add, 0)
-    hop(4, 0)
-    hop(4, 1)
-    lax.fori_loop(14, 16, add, 0)
+        ssq[c] = jnp.sum((xf * xf).reshape(384, 8, 256), axis=0)
+
+    project_own(0)
+    hop(3, 1, 1)
     for dx in (1, 3, 2):
         weight(chunk_at(dx), later, csem, mate).wait_recv()
         to_mate(dx, later).start()
-
-    def add_other(n, carry):
-        zo, c = 2 * lax.rem(n // 2, 4) + lax.rem(core + n // 8, 2), lax.rem(n, 2)
-
-        @pl.when((n >= 8) & (c == 0))
-        def _():
-            for g in range(2):
-                weight(zo, g, csem, mate).wait_recv()
-
-        acc[1, c] += nn(wb[zo], buf[zo, c].reshape(384, 256))
-        return carry
-
-    lax.fori_loop(0, 16, add_other, 0)
+    hop(4, 0, 1)
+    hop(4, 1, 1)
+    project_own(1)
+    for n in range(4):
+        for g in range(2):
+            weight(2 * n + 1 - core, g, csem, mate).wait_recv()
+
+    def project_other(c, carry):
+        acc[1, c] = nn(wb[...], buf[c].reshape(3072, 256))
+        return carry
+
+    lax.fori_loop(0, 2, project_other, 0)
     rates.wait_recv()
     position = lax.broadcasted_iota(jnp.int32, (1, 128), 1)
 
@@ -290,7 +291,7 @@
             source_rate = rate if g == 0 else rate2
             for half in range(2):
                 video = 4 * y + 2 * c + half
-                usable = (position >= 64) | (position < lengths[video, 0])
+                usable = (position >= 64) | (position < lengths[0, video])
                 for h in range(3):
                     slot = item_of(2 * c + half, y if g == 0 else other, h)
                     out[slot, 0:192, :] = projected[
@@ -373,12 +374,12 @@
         ],
         out_specs=(VMEM_SPEC, VMEM_SPEC),
         scratch_shapes=[
-            pltpu.VMEM((8, 2, 2, 192, 256), BF),
+            pltpu.VMEM((2, 8, 2, 192, 256), BF),
             pltpu.VMEM((2, 192, 256), BF),
             pltpu.VMEM((2, 2, 576, 256), F32),
             pltpu.VMEM((2, 8, 256), F32),
             pltpu.VMEM((576, 3072), BF),
-            pltpu.VMEM((8, 576, 384), BF),
+            pltpu.VMEM((576, 3072), BF),
             pltpu.VMEM((3, 8, 128), F32),
             dma,
             dma((6,)),
@@ -672,7 +673,7 @@
         return jnp.swapaxes(array, 1, 2)
 
     items, wsel = gather_project(
-        prompt_len,
+        jnp.swapaxes(prompt_len, 0, 1),
         turned(attn_query),
         turned(attn_key),
         turned(attn_value),

time: 153 us -> 153 us (level)
  Pallas kernels: 149 us -> 151 us
    pallas_call x1, Pallas kernels: 68.8 us -> 70.5 us  [gather_project(): pl.pallas_call(gather_kernel, out_shape=(jax.ShapeDtypeStruct((24, 208, 1...]
    unnamed x2 -> x1, local copies, waits for them, and re-layouts: 3.09 us -> 1.77 us
where the time goes in v6:
time: 153 us; the launch traced here: 152 us
  Pallas kernels  151 us (99%)
  local copies, waits for them, and re-layouts  1.77 us (1%)
    pallas_call x1, Pallas kernels, run_scan(): pl.pallas_call(scan_kernel, out_shape=jax.ShapeDtypeStruct((8, 192, 128),...  80.1 us
    pallas_call x1, Pallas kernels, gather_project(): pl.pallas_call(gather_kernel, out_shape=(jax.ShapeDtypeStruct((24, 208, 1...  70.5 us

profile of v6, /device:TPU:63, one launch (start us, length us, event | category | flops | bytes accessed | tf_op | source)
XLA Modules:
  0.0 152.4 jit_solution(15104194373579790424)
XLA Ops:
  0.0 70.5 %attend_gather_project.1 = (bf16[24,208,128]{2,1,0:T(8,128)(2,1)}, f32[2,64,256]{2,1,0:T(8,128)}) custom-call(s32[1,8]{1,0:T(1,128)} %bitcast.13, bf16[8,192,128]{2,1,0:T(8,128)(2,1)} %bitcast.9, bf16[8,192,128]{2,1,0:T(8,128)(2,1)} %bitcast.10, bf16[8,192,128]{2,1,0:T(8,128)(2,1)} %bitcast.11, bf16[576,3072]{1,0:T(8,128)(2,1)} %bitcast.7, ...), custom_call_target="tpu_custom_call" | custom-call | tf_op jit(solution)/shard_map/attend_gather_project/pallas_call | solution.py:359
  70.5 80.1 %ttt_scan.1 = bf16[8,192,128]{2,1,0:T(8,128)(2,1)} custom-call(bf16[24,208,128]{2,1,0:T(8,128)(2,1)} %get-tuple-element.7.items, f32[2,64,256]{2,1,0:T(8,128)} %get-tuple-element.8.wsel), custom_call_target="tpu_custom_call" | custom-call | tf_op jit(solution)/shard_map/ttt_scan/pallas_call | solution.py:652
  150.6 1.8 %copy.10 = bf16[8,128,192]{1,2,0:T(8,128)(2,1)} copy(bf16[8,128,192]{1,2,0:T(8,128)(2,1)} %bitcast.8) | data formatting | bytes 786432

commit v7 on v6

v7 whole, which is shorter than its diff:
```python
import math

import jax
import jax.numpy as jnp
from jax import lax
from jax.experimental import pallas as pl
from jax.experimental.pallas import tpu as pltpu
from jax.sharding import PartitionSpec as P

F32, BF = jnp.float32, jnp.bfloat16
GC = math.sqrt(2.0 / math.pi)
GA = 0.044715
MESH = pl.DeviceIdType.MESH
VMEM_SPEC = pl.BlockSpec(memory_space=pltpu.VMEM)


def nn(a, b):
    return lax.dot_general(a, b, (((1,), (0,)), ((), ())), preferred_element_type=F32)


def nt(a, b):
    return lax.dot_general(a, b, (((1,), (1,)), ((), ())), preferred_element_type=F32)


def tn(a, b):
    return lax.dot_general(a, b, (((0,), (0,)), ((), ())), preferred_element_type=F32)


def attend(q, k, v, length, put):
    position = lax.broadcasted_iota(jnp.int32, (128, 1), 0)
    usable = (position >= 64) | (position < length)
    for h in range(3):
        rows = slice(64 * h, 64 * h + 64)
        scores = tn(k[rows, :], q[rows, :]) * 0.125
        scores = jnp.where(usable, scores, -1e30)
        exponent = jnp.exp(scores - jnp.max(scores, axis=0, keepdims=True))
        weights = (exponent * (1.0 / jnp.sum(exponent, axis=0, keepdims=True))).astype(BF)
        put(h, nn(v[rows, :], weights).astype(BF))


def forward(u, w2b, xt, st):
    sq = u * u
    t = jnp.tanh(u * (GC + (GC * GA) * sq))
    half = 0.5 + 0.5 * t
    hb = (u * half).astype(BF)
    z = nn(w2b, hb)
    center = z - jnp.mean(z, axis=0, keepdims=True)
    rs = lax.rsqrt(jnp.mean(center * center, axis=0, keepdims=True) + 1e-5)
    y = center * rs
    return sq, t, half, hb, rs, y, y + (xt - st)


def scan_items(get, put, ready, leave, w10, w2t0, w1s, w2s, w2ts, ub, xs, rprev, count):
    left = lax.broadcasted_iota(jnp.int32, (64, 128), 1) < 64
    left1 = lax.broadcasted_iota(jnp.int32, (1, 128), 1) < 64
    zero = jnp.zeros((64, 128), F32)
    zero1 = jnp.zeros((1, 128), F32)
    w1s[...] = w10.T
    w2s[...] = w2t0
    w2ts[...] = w2t0.T
    ready(0)
    x0 = jnp.where(left, get(0, 64, 64), zero)
    ub[...] = nn(w1s[...].astype(BF), x0.astype(BF))
    xs[...] = x0.T.astype(BF)

    def step(xt, st, eta, xnt):
        xntb = xnt.astype(BF)
        u = ub[...]
        sq, t, half, hb, rs, y, r = forward(u, w2s[...].astype(BF), xt, st)
        dy = r * (eta * (1.0 / 64.0))
        m1 = jnp.mean(dy, axis=0, keepdims=True)
        m2 = jnp.mean(dy * y, axis=0, keepdims=True)
        dzb = (rs * (dy - m1 - y * m2)).astype(BF)
        slope = half + (0.5 * u) * ((1.0 - t * t) * (GC + (3.0 * GC * GA) * sq))
        dub = (nn(w2ts[...].astype(BF), dzb) * slope).astype(BF)
        x = xs[...]
        w1 = w1s[...]
        ub[...] = nn(w1.astype(BF), xntb) - nn(dub, nn(x, xntb).astype(BF))
        w1s[...] = w1 - nn(dub, x)
        w2s[...] -= nt(dzb, hb)
        w2ts[...] -= nt(hb, dzb)
        xs[...] = xnt.T.astype(BF)
        return r

    def segment(s, carry):
        prev = jnp.maximum(s - 1, 0)

        @pl.when(s + 1 < count)
        def _():
            ready(s + 1)

        qs, ks, vs = get(s, 0, 64), get(s, 64, 64), get(s, 128, 64)
        qp = get(prev, 0, 64)
        kn = get(jnp.minimum(s + 1, count - 1), 64, 64)
        rate = get(s, 192, 1)
        mid = jnp.where(left, qs, ks)
        even = step(
            jnp.where(left, ks, qp), jnp.where(left, vs, zero), jnp.where(left1, rate, zero1), mid
        )
        put(prev, jnp.where(left, rprev[...], even).astype(BF))
        rprev[...] = step(
            mid, jnp.where(left, zero, vs), jnp.where(left1, zero1, rate), jnp.where(left, kn, qs)
        )

        @pl.when(s > 0)
        def _():
            leave(prev)

        return carry

    rprev[...] = zero
    lax.fori_loop(0, count, segment, 0)
    last = forward(ub[...], w2s[...].astype(BF), get(count - 1, 0, 64), zero)[-1]
    put(count - 1, jnp.where(left, rprev[...], last).astype(BF))


SCAN_SCRATCH = [
    pltpu.VMEM((256, 64), F32),
    pltpu.VMEM((64, 256), F32),
    pltpu.VMEM((256, 64), F32),
    pltpu.VMEM((256, 128), F32),
    pltpu.VMEM((128, 64), BF),
    pltpu.VMEM((64, 128), F32),
]


def fused_kernel(
    lengths, q, k, v, wt, rate, w1, w2t, res,
    items, wsel, qkv, outs, ssend, qsem, osem, hsem,
    buf, pbuf, acc, ssq, wv, wb, rate2,
    wsem, isem, psem, rsem, lsem, recv, csem, ysend, yrecv, xsem, msem, wrecv, *scratch,
):
    me_h, me_s = lax.axis_index("head"), lax.axis_index("seg")
    z, y = me_h // 2, lax.rem(me_h, 2)
    row, x, core = me_s // 8, lax.rem(me_s // 2, 4), lax.rem(me_s, 2)
    other = 1 - y

    def device(seg, head):
        return {"seg": seg, "head": head}

    right, left = device(me_s, lax.rem(me_h + 2, 16)), device(me_s, lax.rem(me_h + 14, 16))
    partner = device(me_s, 2 * z + other)
    above = device(lax.rem(me_s + 8, 32), 2 * z + lax.rem(y + (row + 1) // 4, 2))
    below = device(lax.rem(me_s + 24, 32), 2 * z + lax.rem(y + (4 - row) // 4, 2))
    xpeer = [device(8 * row + 2 * lax.rem(x + dx, 4) + core, me_h) for dx in (1, 2, 3)]
    mate = device(8 * row + 2 * x + 1 - core, me_h)
    barrier = pltpu.get_barrier_semaphore()

    def greet(n, carry):
        peer = lax.rem(me_s + n, 32)
        for target in (device(peer, me_h), device(peer, 2 * z + other)):
            pl.semaphore_signal(barrier, inc=1, device_id=target, device_id_type=MESH)
        return carry

    lax.fori_loop(1, 32, greet, 0)
    for target in (right, left, partner):
        pl.semaphore_signal(barrier, inc=1, device_id=target, device_id_type=MESH)
    load = pltpu.make_async_copy(wt, wv, wsem)
    load.start()
    pl.semaphore_wait(barrier, 65)

    def remote(src, dst, send, receive, peer):
        return pltpu.make_async_remote_copy(
            src_ref=src, dst_ref=dst, send_sem=send, recv_sem=receive,
            device_id=peer, device_id_type=MESH,
        )

    me = me_s
    own = jnp.minimum(me, 23)
    borrowed = own < 12
    video, head = 4 * y + lax.rem(own, 12) // 3, lax.rem(own, 3)
    group = lax.rem(y + 1 - own // 12, 2)

    def start_weight(n):
        source = w1 if n == 0 else w2t
        return remote(source.at[head], wsel.at[n], isem.at[2 + n], isem.at[n], partner)

    def start_local(n):
        source = w1 if n == 0 else w2t
        return pltpu.make_async_copy(source.at[head], wsel.at[n], isem.at[n])

    rates = remote(rate, rate2, isem.at[4], isem.at[5], partner)
    rates.start()

    for n in range(2):

        @pl.when(borrowed)
        def _():
            start_weight(n).start()

        @pl.when(jnp.logical_not(borrowed))
        def _():
            start_local(n).start()


    def block(zo, c, yo, sem, peer):
        return remote(buf.at[c, zo, yo], buf.at[c, zo, yo], sem, recv.at[zo, c, yo], peer)

    def to_right(zo, c, yo, d, o):
        return block(zo, c, yo, rsem.at[d, o, c], right)

    def to_left(zo, c, yo, d, o):
        return block(zo, c, yo, lsem.at[d, o, c], left)

    def to_partner(c):
        return remote(pbuf.at[c], buf.at[c, z, y], psem.at[c], recv.at[z, c, y], partner)

    zc = 2 * x + core
    lanes = pl.ds(pl.multiple_of(zc * 384, 128), 384)

    def half_of(chunk, g):
        columns = pl.ds(pl.multiple_of(chunk * 384, 128), 384)
        return wb.at[pl.ds(pl.multiple_of(288 * g, 32), 288), columns]

    def cross(g, peer):
        source = wt.at[pl.ds(288 * g, 288), lanes]
        return remote(source, half_of(zc, g), csem, yrecv.at[g], peer)

    def onward(g):
        peer = device(lax.rem(me_s + 8 + 16 * g, 32), me_h)
        return remote(half_of(zc, g), half_of(zc, g), ysend.at[g], yrecv.at[g], peer)

    def weight(chunk, g, sem, peer):
        return remote(half_of(chunk, g), half_of(chunk, g), sem, wrecv.at[chunk, g], peer)

    def chunk_at(dx):
        return 2 * lax.rem(x + dx, 4) + core

    def to_mate(dx, g):
        return weight(chunk_at(dx), g, msem.at[dx, g], mate)

    def spread(g):
        for dx in (1, 3, 2):
            weight(zc, g, xsem.at[dx - 1, g], xpeer[dx - 1]).start()
        to_mate(0, g).start()

    sooner = row // 2
    later = 1 - sooner
    edge = (row == 0) | (row == 3)

    def attend_pair(pair, put_half):
        for half in range(2):
            video = 2 * pair + half

            def put(h, value):
                put_half(slice(64 * h, 64 * h + 64), slice(128 * half, 128 * half + 128), value)

            attend(q[video], k[video], v[video], lengths[0, video], put)

    def hop(d, o, c):
        yo = y if o == 0 else other
        zr, zl = lax.rem(z + 8 - d, 8), lax.rem(z + d, 8)
        if d < 4 or c == 0:
            to_right(zr, c, yo, 0, 0).wait_recv()
        if d < 3 or (d == 3 and c == 0):
            to_right(zr, c, yo, d, o).start()
        if d < 4 or c == 1:
            to_left(zl, c, yo, 0, 0).wait_recv()
        if d < 3 or (d == 3 and c == 1):
            to_left(zl, c, yo, d, o).start()

    def send_own(c):
        to_right(z, c, y, 0, 0).start()
        to_left(z, c, y, 0, 0).start()

    def take_partner(c):
        block(z, c, other, psem.at[c], partner).wait_recv()
        to_right(z, c, other, 0, 1).start()
        to_left(z, c, other, 0, 1).start()

    @pl.when(row == 3)
    def _():
        cross(0, above).start()

    @pl.when(row == 0)
    def _():
        cross(1, below).start()

    def attend_partner(c, carry):
        def put_half(rows, cols, value):
            pbuf[c, rows, cols] = value

        attend_pair(2 * other + c, put_half)

        @pl.when(c == 1)
        def _():
            to_partner(0).start()

        return carry

    lax.fori_loop(0, 2, attend_partner, 0)

    def attend_own(c, carry):
        def put_half(rows, cols, value):
            buf[c, z, y, rows, cols] = value

        attend_pair(2 * y + c, put_half)

        @pl.when(c == 0)
        def _():
            to_partner(1).start()

            @pl.when(edge)
            def _():
                onward(sooner).wait_recv()
                onward(sooner).start()
                spread(sooner)

        @pl.when(c == 1)
        def _():
            send_own(0)

        return carry

    lax.fori_loop(0, 2, attend_own, 0)
    load.wait()
    acc[...] = jnp.zeros((2, 2, 576, 256), F32)
    send_own(1)
    hop(1, 0, 0)
    hop(1, 0, 1)

    @pl.when(jnp.logical_not(edge))
    def _():
        onward(sooner).wait_recv()
        onward(sooner).start()
        spread(sooner)

    hop(2, 0, 0)
    take_partner(0)
    hop(2, 0, 1)

    @pl.when(jnp.logical_not(edge))
    def _():
        onward(later).wait_recv()
        onward(later).start()
        spread(later)

    hop(3, 0, 0)
    hop(1, 1, 0)
    hop(3, 0, 1)
    take_partner(1)
    hop(2, 1, 0)

    @pl.when(edge)
    def _():
        onward(later).wait_recv()
        spread(later)

    hop(1, 1, 1)
    for dx in (1, 3, 2):
        weight(chunk_at(dx), sooner, csem, mate).wait_recv()
        to_mate(dx, sooner).start()
    hop(3, 1, 0)
    hop(2, 1, 1)
    hop(4, 0, 0)
    hop(4, 1, 0)

    def item_out(i):
        return pltpu.make_async_remote_copy(
            src_ref=items.at[i],
            dst_ref=qkv.at[me],
            send_sem=ssend.at[i],
            recv_sem=qsem.at[me],
            device_id={"seg": i, "head": me_h},
            device_id_type=MESH,
        )

    def item_in(s):
        return pltpu.make_async_remote_copy(
            src_ref=items.at[0],
            dst_ref=qkv.at[s],
            send_sem=ssend.at[0],
            recv_sem=qsem.at[s],
            device_id={"seg": s, "head": me_h},
            device_id_type=MESH,
        )

    def place(v, h):
        return res.at[v, pl.ds(pl.multiple_of(64 * h, 64), 64), :]

    def item_own():
        return pltpu.make_async_copy(items.at[own], qkv.at[own], qsem.at[own])

    def home(s):
        return pltpu.make_async_remote_copy(
            src_ref=outs.at[s],
            dst_ref=place(video, head),
            send_sem=osem.at[s],
            recv_sem=hsem.at[video * 3 + head],
            device_id={"seg": s, "head": 2 * z + group},
            device_id_type=MESH,
        )

    def home_own():
        return pltpu.make_async_copy(outs.at[own], place(video, head), hsem.at[video * 3 + head])

    def home_in(n):
        return pltpu.make_async_remote_copy(
            src_ref=outs.at[0],
            dst_ref=place(n // 3, lax.rem(n, 3)),
            send_sem=osem.at[0],
            recv_sem=hsem.at[n],
            device_id={"seg": me, "head": 2 * z + 1 - y},
            device_id_type=MESH,
        )

    def stays(s):
        return (s == me) & (group == y)

    position = lax.broadcasted_iota(jnp.int32, (1, 128), 1)

    def finish(g, c):
        mean = jnp.sum(ssq[c], axis=0, keepdims=True) * (1.0 / 3072.0)
        projected = (acc[g, c] * lax.rsqrt(mean + 1e-6)).astype(BF)
        source_rate = rate if g == 0 else rate2
        for half in range(2):
            at = 4 * y + 2 * c + half
            usable = (position >= 64) | (position < lengths[0, at])
            for h in range(3):
                slot = (12 if g == 0 else 0) + (2 * c + half) * 3 + h
                items[slot, 0:192, :] = projected[
                    192 * h : 192 * h + 192, 128 * half : 128 * half + 128
                ]
                eta = jnp.where(usable, source_rate[h, pl.ds(at, 1), :], 0.0)
                items[slot, 192:208, :] = jnp.broadcast_to(eta, (16, 128)).astype(BF)

    def send_items(g, c):
        def send(n, carry):
            i = (12 if g == 0 else 0) + 6 * c + lax.rem(me + n, 6)

            @pl.when(i != me)
            def _():
                item_out(i).start()

            @pl.when(i == me)
            def _():
                item_own().start()

            return carry

        lax.fori_loop(0, 6, send, 0)

    def project_own(c):
        xb = buf[c].reshape(3072, 256)
        acc[0, c] = nn(wv[...], xb)
        xf = xb.astype(F32)
        ssq[c] = jnp.sum((xf * xf).reshape(384, 8, 256), axis=0)

    def project_other(c):
        acc[1, c] = nn(wb[...], buf[c].reshape(3072, 256))

    project_own(0)
    finish(0, 0)
    hop(3, 1, 1)
    for dx in (1, 3, 2):
        weight(chunk_at(dx), later, csem, mate).wait_recv()
        to_mate(dx, later).start()
    send_items(0, 0)
    hop(4, 0, 1)
    hop(4, 1, 1)
    project_own(1)
    finish(0, 1)
    rates.wait_recv()
    for n in range(4):
        for g in range(2):
            weight(2 * n + 1 - core, g, csem, mate).wait_recv()
        if n == 0:
            send_items(0, 1)
    project_other(0)
    finish(1, 0)
    project_other(1)
    send_items(1, 0)
    finish(1, 1)


    def drain(c, carry):
        to_partner(c).wait_send()
        for o in range(2):
            for d in range(3):
                to_right(z, c, y, d, o).wait_send()
                to_left(z, c, y, d, o).wait_send()

            @pl.when(c == 0)
            def _():
                to_right(z, c, y, 3, o).wait_send()

            @pl.when(c == 1)
            def _():
                to_left(z, c, y, 3, o).wait_send()

        return carry

    lax.fori_loop(0, 2, drain, 0)
    send_items(1, 1)

    for n in range(2):

        @pl.when(borrowed)
        def _():
            start_weight(n).wait_recv()

        @pl.when(jnp.logical_not(borrowed))
        def _():
            start_local(n).wait()

    def leave_home(s):
        @pl.when(stays(s))
        def _():
            home_own().start()

        @pl.when(jnp.logical_not(stays(s)))
        def _():
            home(s).start()

    @pl.when(me < 24)
    def _():
        def get(s, row, rows):
            return qkv[s, row : row + rows, :].astype(F32)

        def put(s, value):
            outs[s] = value

        def ready(s):
            @pl.when(s == me)
            def _():
                item_own().wait()

            @pl.when(s != me)
            def _():
                item_in(s).wait_recv()

        scan_items(get, put, ready, leave_home, wsel[0], wsel[1], *scratch, 32)

    def drain_sends(i, carry):
        @pl.when(i != me)
        def _():
            item_out(i).wait_send()

        return carry

    lax.fori_loop(0, 24, drain_sends, 0)

    @pl.when(me < 24)
    def _():
        leave_home(31)

    mine = (me < 24) & (group == y)

    def drain_items(n, carry):
        local = mine & (n == video * 3 + head)

        @pl.when(local)
        def _():
            home_own().wait()

        @pl.when(jnp.logical_not(local))
        def _():
            home_in(n).wait_recv()

        return carry

    lax.fori_loop(0, 24, drain_items, 0)

    @pl.when(me < 24)
    def _():
        def drain_homes(s, carry):
            @pl.when(jnp.logical_not(stays(s)))
            def _():
                home(s).wait_send()

            return carry

        lax.fori_loop(0, 32, drain_homes, 0)

    rates.wait_send()

    for n in range(2):

        @pl.when(borrowed)
        def _():
            start_weight(n).wait_send()

    @pl.when(edge)
    def _():
        cross(0, above).wait_send()

    onward(sooner).wait_send()

    @pl.when(jnp.logical_not(edge))
    def _():
        onward(later).wait_send()

    for g in range(2):
        for dx in range(4):
            to_mate(dx, g).wait_send()
        for dx in range(3):
            weight(zc, g, xsem.at[dx, g], xpeer[dx]).wait_send()


def fused(lengths, q, k, v, wt, rate, w1, w2t):
    any_spec = pl.BlockSpec(memory_space=pl.ANY)
    dma = pltpu.SemaphoreType.DMA
    return pl.pallas_call(
        fused_kernel,
        out_shape=jax.ShapeDtypeStruct((8, 192, 128), BF),
        in_specs=[
            pl.BlockSpec(memory_space=pltpu.SMEM),
            VMEM_SPEC,
            VMEM_SPEC,
            VMEM_SPEC,
            any_spec,
            VMEM_SPEC,
            VMEM_SPEC,
            VMEM_SPEC,
        ],
        out_specs=VMEM_SPEC,
        scratch_shapes=[
            pltpu.VMEM((24, 208, 128), BF),
            pltpu.VMEM((2, 64, 256), F32),
            pltpu.VMEM((32, 208, 128), BF),
            pltpu.VMEM((32, 64, 128), BF),
            dma((24,)),
            dma((32,)),
            dma((32,)),
            dma((24,)),
            pltpu.VMEM((2, 8, 2, 192, 256), BF),
            pltpu.VMEM((2, 192, 256), BF),
            pltpu.VMEM((2, 2, 576, 256), F32),
            pltpu.VMEM((2, 8, 256), F32),
            pltpu.VMEM((576, 3072), BF),
            pltpu.VMEM((576, 3072), BF),
            pltpu.VMEM((3, 8, 128), F32),
            dma,
            dma((6,)),
            dma((2,)),
            dma((4, 2, 2)),
            dma((4, 2, 2)),
            dma((8, 2, 2)),
            dma,
            dma((2,)),
            dma((2,)),
            dma((3, 2)),
            dma((4, 2)),
            dma((8, 2)),
        ]
        + SCAN_SCRATCH,
        compiler_params=pltpu.CompilerParams(
            collective_id=0, has_side_effects=True, vmem_limit_bytes=56 << 20
        ),
        name="attend_gather_scan",
    )(lengths, q, k, v, wt, rate, w1, w2t)


def body(attn_query, attn_key, attn_value, prompt_len, ttt_weight, init_w1, init_w2t, step_rate):
    def turned(array):
        return jnp.swapaxes(array, 1, 2)

    results = fused(
        jnp.swapaxes(prompt_len, 0, 1),
        turned(attn_query),
        turned(attn_key),
        turned(attn_value),
        ttt_weight.T,
        jnp.swapaxes(step_rate, 0, 1),
        init_w1,
        init_w2t,
    )
    return turned(results)


def solution(mesh):
    in_specs = (
        P(None, "seg", "head"),
        P(None, "seg", "head"),
        P(None, "seg", "head"),
        P(None, "seg"),
        P(None, "head"),
        P("head", None, None),
        P("head", None, None),
        P(None, "head", "seg"),
    )
    return jax.shard_map(
        body, mesh=mesh, in_specs=in_specs, out_specs=P(None, "seg", "head"), check_vma=False
    )
```

time: 153 us -> 141 us (0.922)
  the two profiles are of different devices: /device:TPU:63 before, /device:TPU:31 now
where the time goes in v7:
time: 141 us
  Pallas kernels  139 us (99%)
  local copies, waits for them, and re-layouts  1.77 us (1%)
    pallas_call x1, Pallas kernels, fused(): pl.pallas_call(fused_kernel, out_shape=jax.ShapeDtypeStruct((8, 192, 128)...  139 us

profile of v7, /device:TPU:31, one launch (start us, length us, event | category | flops | bytes accessed | tf_op | source)
XLA Modules:
  0.0 140.5 jit_solution(2639057487833228979)
XLA Ops:
  0.0 138.7 %attend_gather_scan.1 = bf16[8,192,128]{2,1,0:T(8,128)(2,1)} custom-call(s32[1,8]{1,0:T(1,128)} %bitcast.13, bf16[8,192,128]{2,1,0:T(8,128)(2,1)} %bitcast.9, bf16[8,192,128]{2,1,0:T(8,128)(2,1)} %bitcast.10, bf16[8,192,128]{2,1,0:T(8,128)(2,1)} %bitcast.11, bf16[576,3072]{1,0:T(8,128)(2,1)} %bitcast.7, f32[3,8,128]{2,1,0:T(8,128)} %bitcast.12, ...), custom_call_target="tpu_custom_call" | custom-call | tf_op jit(solution)/shard_map/attend_gather_scan/pallas_call | solution.py:603
  138.7 1.8 %copy.10 = bf16[8,128,192]{1,2,0:T(8,128)(2,1)} copy(bf16[8,128,192]{1,2,0:T(8,128)(2,1)} %bitcast.8) | data formatting | bytes 786432

commit v8 on v7

--- a/solution.py
+++ b/solution.py
@@ -128,7 +128,7 @@
     lengths, q, k, v, wt, rate, w1, w2t, res,
     items, wsel, qkv, outs, ssend, qsem, osem, hsem,
     buf, pbuf, acc, ssq, wv, wb, rate2,
-    wsem, isem, psem, rsem, lsem, recv, csem, ysend, yrecv, xsem, msem, wrecv, *scratch,
+    wsem, isem, psem, rsem, lsem, recv, csem, ysend, yrecv, xsem, qsend, qrecv, msem, wrecv, *scratch,
 ):
     me_h, me_s = lax.axis_index("head"), lax.axis_index("seg")
     z, y = me_h // 2, lax.rem(me_h, 2)
@@ -230,9 +230,26 @@
         return weight(chunk_at(dx), g, msem.at[dx, g], mate)
 
     def spread(g):
-        for dx in (1, 3, 2):
-            weight(zc, g, xsem.at[dx - 1, g], xpeer[dx - 1]).start()
+        weight(zc, g, xsem.at[0, g], xpeer[0]).start()
+        weight(zc, g, xsem.at[1, g], xpeer[2]).start()
         to_mate(0, g).start()
+
+    def quarter(way, g, dx=None):
+        chunk = chunk_at((3, 1)[way] if dx is None else dx)
+        columns = pl.ds(pl.multiple_of(chunk * 384, 128), 384)
+        part = wb.at[pl.ds(pl.multiple_of(288 * g + 144 * way, 16), 144), columns]
+        return remote(part, part, qsend.at[way, g], qrecv.at[way, g], xpeer[2 * way])
+
+    def pass_on(g):
+        for way, dx in ((0, 3), (1, 1)):
+            weight(chunk_at(dx), g, csem, mate).wait_recv()
+            quarter(way, g).start()
+            to_mate(dx, g).start()
+
+    def take_far(g):
+        for way in range(2):
+            quarter(way, g, 2).wait_recv()
+        to_mate(2, g).start()
 
     sooner = row // 2
     later = 1 - sooner
@@ -276,29 +293,18 @@
     def _():
         cross(1, below).start()
 
-    def attend_partner(c, carry):
-        def put_half(rows, cols, value):
+    def attend_both(c, carry):
+        def put_own(rows, cols, value):
+            buf[c, z, y, rows, cols] = value
+
+        def put_partner(rows, cols, value):
             pbuf[c, rows, cols] = value
 
-        attend_pair(2 * other + c, put_half)
+        attend_pair(2 * y + c, put_own)
 
         @pl.when(c == 1)
         def _():
             to_partner(0).start()
-
-        return carry
-
-    lax.fori_loop(0, 2, attend_partner, 0)
-
-    def attend_own(c, carry):
-        def put_half(rows, cols, value):
-            buf[c, z, y, rows, cols] = value
-
-        attend_pair(2 * y + c, put_half)
-
-        @pl.when(c == 0)
-        def _():
-            to_partner(1).start()
 
             @pl.when(edge)
             def _():
@@ -306,18 +312,17 @@
                 onward(sooner).start()
                 spread(sooner)
 
-        @pl.when(c == 1)
-        def _():
-            send_own(0)
-
+        attend_pair(2 * other + c, put_partner)
+        send_own(c)
         return carry
 
-    lax.fori_loop(0, 2, attend_own, 0)
+    lax.fori_loop(0, 2, attend_both, 0)
     load.wait()
     acc[...] = jnp.zeros((2, 2, 576, 256), F32)
-    send_own(1)
+    to_partner(1).start()
     hop(1, 0, 0)
     hop(1, 0, 1)
+    hop(2, 0, 0)
 
     @pl.when(jnp.logical_not(edge))
     def _():
@@ -325,9 +330,10 @@
         onward(sooner).start()
         spread(sooner)
 
-    hop(2, 0, 0)
+    hop(2, 0, 1)
+    hop(3, 0, 0)
     take_partner(0)
-    hop(2, 0, 1)
+    hop(3, 0, 1)
 
     @pl.when(jnp.logical_not(edge))
     def _():
@@ -335,9 +341,8 @@
         onward(later).start()
         spread(later)
 
-    hop(3, 0, 0)
     hop(1, 1, 0)
-    hop(3, 0, 1)
+    pass_on(sooner)
     take_partner(1)
     hop(2, 1, 0)
 
@@ -347,13 +352,12 @@
         spread(later)
 
     hop(1, 1, 1)
-    for dx in (1, 3, 2):
-        weight(chunk_at(dx), sooner, csem, mate).wait_recv()
-        to_mate(dx, sooner).start()
+    take_far(sooner)
     hop(3, 1, 0)
     hop(2, 1, 1)
     hop(4, 0, 0)
     hop(4, 1, 0)
+    pass_on(later)
 
     def item_out(i):
         return pltpu.make_async_remote_copy(
@@ -446,29 +450,33 @@
         xf = xb.astype(F32)
         ssq[c] = jnp.sum((xf * xf).reshape(384, 8, 256), axis=0)
 
-    def project_other(c):
-        acc[1, c] = nn(wb[...], buf[c].reshape(3072, 256))
-
+    def project_other(g, c):
+        rows = pl.ds(pl.multiple_of(288 * g, 32), 288)
+        acc[1, c, rows, :] = nn(wb[rows, :], buf[c].reshape(3072, 256))
+
+    def from_mate(n, g):
+        weight(2 * n + 1 - core, g, csem, mate).wait_recv()
+
+    hop(3, 1, 1)
     project_own(0)
     finish(0, 0)
-    hop(3, 1, 1)
-    for dx in (1, 3, 2):
-        weight(chunk_at(dx), later, csem, mate).wait_recv()
-        to_mate(dx, later).start()
+    take_far(later)
     send_items(0, 0)
+    for n in range(4):
+        from_mate(n, sooner)
+    project_other(sooner, 0)
     hop(4, 0, 1)
     hop(4, 1, 1)
     project_own(1)
     finish(0, 1)
+    project_other(sooner, 1)
+    send_items(0, 1)
     rates.wait_recv()
     for n in range(4):
-        for g in range(2):
-            weight(2 * n + 1 - core, g, csem, mate).wait_recv()
-        if n == 0:
-            send_items(0, 1)
-    project_other(0)
+        from_mate(n, later)
+    project_other(later, 0)
     finish(1, 0)
-    project_other(1)
+    project_other(later, 1)
     send_items(1, 0)
     finish(1, 1)
 
@@ -593,8 +601,9 @@
     for g in range(2):
         for dx in range(4):
             to_mate(dx, g).wait_send()
-        for dx in range(3):
-            weight(zc, g, xsem.at[dx, g], xpeer[dx]).wait_send()
+        for way in range(2):
+            weight(zc, g, xsem.at[way, g], xpeer[2 * way]).wait_send()
+            quarter(way, g).wait_send()
 
 
 def fused(lengths, q, k, v, wt, rate, w1, w2t):
@@ -639,7 +648,9 @@
             dma,
             dma((2,)),
             dma((2,)),
-            dma((3, 2)),
+            dma((2, 2)),
+            dma((2, 2)),
+            dma((2, 2)),
             dma((4, 2)),
             dma((8, 2)),
         ]

time: 141 us -> 142 us (level)
  the two profiles are of different devices: /device:TPU:31 before, /device:TPU:63 now
where the time goes in v8:
time: 142 us
  Pallas kernels  140 us (99%)
  local copies, waits for them, and re-layouts  1.77 us (1%)
    pallas_call x1, Pallas kernels, fused(): pl.pallas_call(fused_kernel, out_shape=jax.ShapeDtypeStruct((8, 192, 128)...  140 us

profile of v8, /device:TPU:63, one launch (start us, length us, event | category | flops | bytes accessed | tf_op | source)
XLA Modules:
  0.0 141.9 jit_solution(17877379953613140246)
XLA Ops:
  0.0 140.1 %attend_gather_scan.1 = bf16[8,192,128]{2,1,0:T(8,128)(2,1)} custom-call(s32[1,8]{1,0:T(1,128)} %bitcast.13, bf16[8,192,128]{2,1,0:T(8,128)(2,1)} %bitcast.9, bf16[8,192,128]{2,1,0:T(8,128)(2,1)} %bitcast.10, bf16[8,192,128]{2,1,0:T(8,128)(2,1)} %bitcast.11, bf16[576,3072]{1,0:T(8,128)(2,1)} %bitcast.7, f32[3,8,128]{2,1,0:T(8,128)} %bitcast.12, ...), custom_call_target="tpu_custom_call" | custom-call | tf_op jit(solution)/shard_map/attend_gather_scan/pallas_call | solution.py:612
  140.1 1.8 %copy.10 = bf16[8,128,192]{1,2,0:T(8,128)(2,1)} copy(bf16[8,128,192]{1,2,0:T(8,128)(2,1)} %bitcast.8) | data formatting | bytes 786432

commit v9 on v7

--- a/solution.py
+++ b/solution.py
@@ -126,7 +126,7 @@
 
 def fused_kernel(
     lengths, q, k, v, wt, rate, w1, w2t, res,
-    items, wsel, qkv, outs, ssend, qsem, osem, hsem,
+    items, wsel, qkv, outs, ssend, qsem, osem, hsem, go,
     buf, pbuf, acc, ssq, wv, wb, rate2,
     wsem, isem, psem, rsem, lsem, recv, csem, ysend, yrecv, xsem, msem, wrecv, *scratch,
 ):
@@ -469,7 +469,11 @@
     project_other(0)
     finish(1, 0)
     project_other(1)
-    send_items(1, 0)
+
+    @pl.when(row < 2)
+    def _():
+        send_items(1, 0)
+
     finish(1, 1)
 
 
@@ -491,6 +495,12 @@
         return carry
 
     lax.fori_loop(0, 2, drain, 0)
+
+    @pl.when(row >= 2)
+    def _():
+        pl.semaphore_wait(go, 1)
+        send_items(1, 0)
+
     send_items(1, 1)
 
     for n in range(2):
@@ -529,7 +539,17 @@
             def _():
                 item_in(s).wait_recv()
 
-        scan_items(get, put, ready, leave_home, wsel[0], wsel[1], *scratch, 32)
+        def leave(s):
+            leave_home(s)
+            for rows, after in ((16, 2), (24, 8)):
+
+                @pl.when((s == after) & (row == 0))
+                def _():
+                    pl.semaphore_signal(
+                        go, inc=1, device_id=device(me + rows, me_h), device_id_type=MESH
+                    )
+
+        scan_items(get, put, ready, leave, wsel[0], wsel[1], *scratch, 32)
 
     def drain_sends(i, carry):
         @pl.when(i != me)
@@ -623,6 +643,7 @@
             dma((32,)),
             dma((32,)),
             dma((24,)),
+            pltpu.SemaphoreType.REGULAR,
             pltpu.VMEM((2, 8, 2, 192, 256), BF),
             pltpu.VMEM((2, 192, 256), BF),
             pltpu.VMEM((2, 2, 576, 256), F32),

time: 141 us -> 149 us (1.057)
  the two profiles are of different devices: /device:TPU:31 before, /device:TPU:63 now
where the time goes in v9:
time: 149 us
  Pallas kernels  147 us (99%)
  local copies, waits for them, and re-layouts  1.77 us (1%)
    pallas_call x1, Pallas kernels, fused(): pl.pallas_call(fused_kernel, out_shape=jax.ShapeDtypeStruct((8, 192, 128)...  147 us

profile of v9, /device:TPU:63, one launch (start us, length us, event | category | flops | bytes accessed | tf_op | source)
XLA Modules:
  0.0 148.5 jit_solution(12349260200110487746)
XLA Ops:
  0.0 146.7 %attend_gather_scan.1 = bf16[8,192,128]{2,1,0:T(8,128)(2,1)} custom-call(s32[1,8]{1,0:T(1,128)} %bitcast.13, bf16[8,192,128]{2,1,0:T(8,128)(2,1)} %bitcast.9, bf16[8,192,128]{2,1,0:T(8,128)(2,1)} %bitcast.10, bf16[8,192,128]{2,1,0:T(8,128)(2,1)} %bitcast.11, bf16[576,3072]{1,0:T(8,128)(2,1)} %bitcast.7, f32[3,8,128]{2,1,0:T(8,128)} %bitcast.12, ...), custom_call_target="tpu_custom_call" | custom-call | tf_op jit(solution)/shard_map/attend_gather_scan/pallas_call | solution.py:623
  146.8 1.8 %copy.10 = bf16[8,128,192]{1,2,0:T(8,128)(2,1)} copy(bf16[8,128,192]{1,2,0:T(8,128)(2,1)} %bitcast.8) | data formatting | bytes 786432
